TPU v7x, 128 devices: a whole 4x4x4 slice. The times are simulated.
128 devices in a mesh: gx: 32 (over x, y, core), gy: 4 (over z).
Axes of the slice: x: 4, y: 4, z: 4, core: 2. Of those that a mesh axis runs over, the one named last changes fastest.
Arguments:
- tokens: bfloat16 [16384, 2048], P(('gx', 'gy')), may hold values from -6 to 6
- expert_ids: int32 [16384, 8], P(('gx', 'gy')), may hold values from 0 to 127, all different within a row; in each aligned block of 128 rows (0 to 127, 128 to 255, ...) at most 24 rows name the same one
- w_gate: bfloat16 [128, 2048, 768], P(('gx', 'gy')), may hold values from -0.125 to 0.125
- w_up: bfloat16 [128, 2048, 768], P(('gx', 'gy')), may hold values from -0.125 to 0.125
- down_error: float32 [128, 768, 2048], P(('gx', 'gy')), may hold values from -18 to 18
Outputs:
- gram_error: float32 [128, 768, 2048], P(('gx', 'gy'))
Inputs may be any that keep to these rules, and one draw needn't show every extreme that they name: `expert_ids`: among the rows of one device no expert is named more than 24 times, a bound that some block reaches; every expert is named by some row; the 8 ids of a row are distinct.
All inputs are finite; a program needn't handle non-finite values.
Results may differ from a plain program's by a relative error of at most 0.0036.
Values may be sent and summed in bfloat16 or wider, within the bound.
No kernel may reach another device: no remote copies, remote signals or barrier semaphores. Data moves between devices by JAX's collectives and lax.ppermute only.
A program may use at most 128 MiB of HBM per device.

v0:
```python
import functools
import itertools

import jax
import jax.numpy as jnp
import numpy as np
from jax import lax
from jax.experimental import pallas as pl
from jax.experimental.pallas import tpu as pltpu
from jax.sharding import PartitionSpec as P

AXES = ("gx", "gy")
FREE = 64.0
LIMIT = 32.0
RING = 4
EXTRA = 8
SENT = [(shift, cross) for shift in range(RING) for cross in range(2)]
COLS = 512


def place(x, y, c, z):
    return ((x % RING * RING + y % RING) * 2 + c) * RING + z % RING


SPOTS = list(itertools.product(range(RING), range(RING), range(2), range(RING)))


def owner(shift, cross, x, y, c, z):
    return place(x + shift, y, c ^ cross, z) if c else place(x, y, c ^ cross, z + shift)


TARGETS = np.array([[owner(*sent, *spot) for sent in SENT] for spot in SPOTS], np.int32)


def along_y(shift):
    return [(place(x, y, c, z), place(x, y + shift, c, z)) for x, y, c, z in SPOTS]


def gather_ring(shift):
    return [
        (place(x, y, c, z), place(x, y, c, z + shift) if c else place(x + shift, y, c, z))
        for x, y, c, z in SPOTS
    ]


def owner_ring(shift):
    return [(place(*spot), owner(shift, 0, *spot)) for spot in SPOTS]


OTHER_CORE = [(place(x, y, c, z), place(x, y, 1 - c, z)) for x, y, c, z in SPOTS]


def move(value, route, name="y"):
    with jax.named_scope(name):
        return lax.ppermute(value, AXES, route)


def tie(*values):
    return lax.optimization_barrier(values)


def pack_kernel(slots, experts_ref, *refs):
    ins, outs = refs[:-RING], refs[-RING:]
    tokens = ins[0].shape[1]
    width = outs[0].shape[2]
    group = len(SENT)
    top = experts_ref.shape[0]
    experts = experts_ref[...].astype(jnp.float32)
    before = (
        lax.broadcasted_iota(jnp.int32, (tokens, tokens), 0)
        < lax.broadcasted_iota(jnp.int32, (tokens, tokens), 1)
    ).astype(jnp.bfloat16)
    slot = lax.broadcasted_iota(jnp.int32, (group, slots, tokens), 1).astype(jnp.float32)
    lane = lax.broadcasted_iota(jnp.int32, (group, slots, tokens), 2)
    at = 0
    for ref in ins:
        for b in range(ref.shape[0]):
            ids = ref[b, :top, width:].astype(jnp.float32)
            member = jnp.zeros((group, tokens), jnp.float32)
            for k in range(top):
                member += (ids[k : k + 1, :] == experts).astype(jnp.float32)
            rank = jnp.dot(member.astype(jnp.bfloat16), before, preferred_element_type=jnp.float32)
            rank = jnp.where(member > 0.5, rank, -1.0)
            total = jnp.sum(member, axis=1, keepdims=True)
            picks = (rank[:, None, :] == slot).astype(jnp.float32)
            picks = picks.reshape(group * slots, tokens).astype(jnp.bfloat16)
            rows = jnp.dot(picks, ref[b, :, :width], preferred_element_type=jnp.float32)
            free = (slot >= total[:, :, None]) & (lane == 0)
            mark = jnp.where(free, FREE, 0.0).reshape(group * slots, tokens)
            for g, (shift, cross) in enumerate(SENT):
                here = slice(g * slots, (g + 1) * slots)
                spot = slice(at * slots, (at + 1) * slots)
                out = outs[shift]
                out[cross, spot, :tokens] = (rows[here, :tokens] + mark[here]).astype(jnp.bfloat16)
                out[cross, spot, tokens:] = rows[here, tokens:].astype(jnp.bfloat16)
            at += 1


def pack(slots, width, experts, parts):
    blocks = sum(part.shape[0] for part in parts)
    shape = jax.ShapeDtypeStruct((2, blocks * slots, width), jnp.bfloat16)
    tokens = parts[0].shape[1]
    rows = len(SENT) * blocks * slots
    return pl.pallas_call(
        functools.partial(pack_kernel, slots),
        out_shape=[shape] * RING,
        in_specs=[pl.BlockSpec(memory_space=pltpu.VMEM)] * (1 + len(parts)),
        out_specs=[pl.BlockSpec(memory_space=pltpu.VMEM)] * RING,
        compiler_params=pltpu.CompilerParams(vmem_limit_bytes=24 << 20),
        cost_estimate=pl.CostEstimate(
            flops=2 * rows * tokens * width,
            transcendentals=0,
            bytes_accessed=2 * rows * width + 2 * blocks * tokens * width,
        ),
        name="pack_rows",
    )(experts, *parts)


def consume_kernel(which, more, *refs):
    rows, (wg, wu), refs = refs[:RING], refs[RING : RING + 2], refs[RING + 2 :]
    if more:
        before_ref, refs = refs[0], refs[1:]
    sum_ref, sem, x, h = refs
    n = rows[0].shape[1]
    ff = h.shape[1]
    copies = [
        pltpu.make_async_copy(rows[j].at[which], x.at[pl.ds(j * n, n)], sem.at[j])
        for j in range(RING)
    ]
    for copy in copies:
        copy.start()
    count = before_ref[ff:, :1] if more else jnp.zeros((EXTRA, 1), jnp.float32)
    group = RING if n < 128 else 2
    for j in range(0, RING, group):
        for copy in copies[j : j + group]:
            copy.wait()
        tile = x[pl.ds(j * n, group * n), :]
        gate = jnp.dot(tile, wg[0], preferred_element_type=jnp.float32)
        upward = jnp.dot(tile, wu[0], preferred_element_type=jnp.float32)
        live = tile[:, :1].astype(jnp.float32) < LIMIT
        hidden = gate / (1.0 + jnp.exp(-gate)) * upward
        h[pl.ds(j * n, group * n), :] = jnp.where(live, hidden, 0.0).astype(jnp.bfloat16)
        count += jnp.sum(live.astype(jnp.float32), axis=0, keepdims=True)
    gram = lax.dot_general(
        h[...], h[...], (((0,), (0,)), ((), ())), preferred_element_type=jnp.float32
    )
    sum_ref[:ff, :] = gram + before_ref[:ff, :] if more else gram
    sum_ref[ff:, :] = jnp.broadcast_to(count, (EXTRA, ff))


def consume(which, rows, w_gate, w_up, before=None):
    _, n, width = rows[0].shape
    ff = w_gate.shape[2]
    total = n * RING
    more = before is not None
    hbm, vmem = pl.BlockSpec(memory_space=pl.ANY), pl.BlockSpec(memory_space=pltpu.VMEM)
    operands = [*rows, w_gate, w_up]
    specs = [hbm] * RING + [vmem] * 2
    if more:
        operands.append(before)
        specs.append(vmem)
    return pl.pallas_call(
        functools.partial(consume_kernel, which, more),
        out_shape=jax.ShapeDtypeStruct((ff + EXTRA, ff), jnp.float32),
        in_specs=specs,
        out_specs=vmem,
        scratch_shapes=[
            pltpu.SemaphoreType.DMA((RING,)),
            pltpu.VMEM((total, width), jnp.bfloat16),
            pltpu.VMEM((total, ff), jnp.bfloat16),
        ],
        compiler_params=pltpu.CompilerParams(vmem_limit_bytes=28 << 20),
        cost_estimate=pl.CostEstimate(
            flops=4 * total * width * ff + 2 * total * ff * ff,
            transcendentals=total * ff,
            bytes_accessed=2 * total * width + 4 * width * ff + 8 * ff * ff,
        ),
        name="hidden_gram",
    )(*operands)


def finish_kernel(one_ref, two_ref, down_ref, out_ref, mean_ref):
    ff = mean_ref.shape[0]

    @pl.when(pl.program_id(0) == 0)
    def _():
        count = one_ref[ff : ff + 1, :1] + two_ref[ff : ff + 1, :1]
        mean = (one_ref[:ff, :] + two_ref[:ff, :]) / count
        mean_ref[...] = mean.astype(jnp.bfloat16)

    down = down_ref[0].astype(jnp.bfloat16)
    out_ref[0] = jnp.dot(mean_ref[...], down, preferred_element_type=jnp.float32)


def finish(one, two, down):
    _, ff, wide = down.shape
    part = pl.BlockSpec((1, ff, COLS), lambda i: (0, 0, i))
    whole = pl.BlockSpec(one.shape, lambda i: (0, 0))
    return pl.pallas_call(
        finish_kernel,
        out_shape=jax.ShapeDtypeStruct(down.shape, jnp.float32),
        grid=(wide // COLS,),
        in_specs=[whole, whole, part],
        out_specs=part,
        scratch_shapes=[pltpu.VMEM((ff, ff), jnp.bfloat16)],
        compiler_params=pltpu.CompilerParams(vmem_limit_bytes=28 << 20),
        name="mean_product",
    )(one, two, down)


def exchange(packed):
    sent = [move(packed[shift], owner_ring(shift), "F") for shift in (2, 1, 3)]
    return [packed[0], *sent]


def local(tokens, expert_ids, w_gate, w_up, down_error):
    experts = lax.axis_size("gx") * lax.axis_size("gy")
    count, top = expert_ids.shape
    width = tokens.shape[1]
    slots = 3 * count * top // experts
    me = lax.axis_index(AXES)
    targets = lax.dynamic_slice(jnp.asarray(TARGETS), (me, 0), (1, len(SENT)))
    targets = jnp.broadcast_to(targets[0][:, None], (len(SENT), count))
    ids = jnp.pad(expert_ids.T.astype(jnp.bfloat16), ((0, count - top), (0, 0)))
    own = jnp.concatenate([tokens, ids], axis=1)[None]

    def packed(*parts):
        return pack(slots, width, targets, parts)

    ring = [move(own, gather_ring(shift), "ring") for shift in (2, 1, -1)]
    own_up, own_down = move(own, along_y(1), "own"), move(own, along_y(-1), "own")
    *ring, own_up, own_down = tie(*ring, own_up, own_down)
    near = jnp.concatenate(ring, axis=0)
    near, own = tie(near, own)
    near_up, near_down = move(near, along_y(1), "near"), move(near, along_y(-1), "near")
    rows_a = exchange(packed(own, *ring, own_up, own_down))
    mine = consume(0, rows_a, w_gate, w_up)
    near_up, near_down, mine, other_gate, other_up, *rows_a = tie(
        near_up, near_down, mine, w_gate, w_up, *rows_a
    )
    other_gate, other_up = move(other_gate, OTHER_CORE, "og"), move(other_up, OTHER_CORE, "ou")
    next_up = jnp.concatenate([own_up, near_up[:1]], axis=0)
    far_up, far_down = move(next_up, along_y(1), "far"), move(near_down[1:], along_y(-1), "far")
    rows_b = exchange(packed(near_up, near_down))
    theirs = consume(1, rows_a, other_gate, other_up)
    far_up, far_down, theirs, *rows_b = tie(far_up, far_down, theirs, *rows_b)
    rows_c = exchange(packed(far_up, far_down))
    mine = consume(0, rows_b, w_gate, w_up, mine)
    theirs = consume(1, rows_b, other_gate, other_up, theirs)
    mine, theirs, *rows_c = tie(mine, theirs, *rows_c)
    theirs = move(consume(1, rows_c, other_gate, other_up, theirs), OTHER_CORE, "sums")
    mine = consume(0, rows_c, w_gate, w_up, mine)
    return finish(mine, theirs, down_error)


def solution(mesh):
    return jax.shard_map(
        local,
        mesh=mesh,
        in_specs=(
            P(AXES, None),
            P(AXES, None),
            P(AXES, None, None),
            P(AXES, None, None),
            P(AXES, None, None),
        ),
        out_specs=P(AXES, None, None),
        check_vma=False,
    )
```

profile of v0, /device:TPU:1, one launch (start us, length us, event | category | flops | bytes accessed | tf_op | source)
XLA Modules:
  0.0 143.8 jit_solution(9684337453542861163)
XLA Ops:
  0.0 0.7 convert_bitcast_fusion
  0.7 1.1 fusion.2.refs_0_
  1.8 4.5 %collective-permute-start = (bf16[1,128,2176]{2,1,0:T(8,128)(2,1)S(1)}, bf16[1,128,2176]{2,1,0:T(8,128)(2,1)S(1)}, u32[]{:S(2)}, u32[]{:S(2)}) collective-permute-start(bf16[1,128,2176]{2,1,0:T(8,128)(2,1)S(1)} %fusion.2.refs_0_), channel_id=1, source_target_pairs={{0,64},{1,65},{2,66},{3,67},{4,6},{5,7},{6,4},{7,5},{8,72},{9,73},... | collective-permute-start | bytes 1671176 | tf_op jit(solution)/shard_map/ring/ppermute | solution.py:55
  6.3 0.7 collective-permute-start.1
  7.0 1.9 %collective-permute-start.2 = (bf16[1,128,2176]{2,1,0:T(8,128)(2,1)S(1)}, bf16[1,128,2176]{2,1,0:T(8,128)(2,1)S(1)}, u32[]{:S(2)}, u32[]{:S(2)}) collective-permute-start(bf16[1,128,2176]{2,1,0:T(8,128)(2,1)S(1)} %fusion.2.refs_0_), channel_id=1, source_target_pairs={{0,96},{1,97},{2,98},{3,99},{4,7},{5,4},{6,5},{7,6},{8,104},{9,105... | collective-permute-start | bytes 1671176 | tf_op jit(solution)/shard_map/ring/ppermute | solution.py:55
  9.0 1.3 collective-permute-start.3
  10.3 1.4 %collective-permute-start.4 = (bf16[1,128,2176]{2,1,0:T(8,128)(2,1)S(1)}, bf16[1,128,2176]{2,1,0:T(8,128)(2,1)S(1)}, u32[]{:S(2)}, u32[]{:S(2)}) collective-permute-start(bf16[1,128,2176]{2,1,0:T(8,128)(2,1)S(1)} %fusion.2.refs_0_), channel_id=1, source_target_pairs={{0,24},{1,25},{2,26},{3,27},{4,28},{5,29},{6,30},{7,31},{8,0},{9,1... | collective-permute-start | bytes 1671176 | tf_op jit(solution)/shard_map/own/ppermute | solution.py:55
  11.7 1.8 %collective-permute-done.refs_1_ = bf16[1,128,2176]{2,1,0:T(8,128)(2,1)S(1)} collective-permute-done((bf16[1,128,2176]{2,1,0:T(8,128)(2,1)S(1)}, bf16[1,128,2176]{2,1,0:T(8,128)(2,1)S(1)}, u32[]{:S(2)}, u32[]{:S(2)}) %collective-permute-start) | collective-permute-done | bytes 557088 | tf_op jit(solution)/shard_map/ring/ppermute | solution.py:55
  13.5 5.9 %collective-permute-done.1.refs_2_ = bf16[1,128,2176]{2,1,0:T(8,128)(2,1)S(1)} collective-permute-done((bf16[1,128,2176]{2,1,0:T(8,128)(2,1)S(1)}, bf16[1,128,2176]{2,1,0:T(8,128)(2,1)S(1)}, u32[]{:S(2)}, u32[]{:S(2)}) %collective-permute-start.1) | collective-permute-done | bytes 557088 | tf_op jit(solution)/shard_map/ring/ppermute | solution.py:55
  19.5 0.8 collective-permute-done.2.refs_3_
  20.2 3.6 %collective-permute-done.3.refs_4_ = bf16[1,128,2176]{2,1,0:T(8,128)(2,1)S(1)} collective-permute-done((bf16[1,128,2176]{2,1,0:T(8,128)(2,1)S(1)}, bf16[1,128,2176]{2,1,0:T(8,128)(2,1)S(1)}, u32[]{:S(2)}, u32[]{:S(2)}) %collective-permute-start.3) | collective-permute-done | bytes 557088 | tf_op jit(solution)/shard_map/own/ppermute | solution.py:55
  23.8 0.0 collective-permute-done.4.refs_5_
  23.8 0.2 pad_maximum_fusion
  24.0 1.0 collective-permute-start.5
  25.0 1.7 %collective-permute-start.6 = (bf16[3,128,2176]{2,1,0:T(8,128)(2,1)S(1)}, bf16[3,128,2176]{2,1,0:T(8,128)(2,1)S(1)}, u32[]{:S(2)}, u32[]{:S(2)}) collective-permute-start(bf16[3,128,2176]{2,1,0:T(8,128)(2,1)S(1)} %pad_maximum_fusion), channel_id=1, source_target_pairs={{0,24},{1,25},{2,26},{3,27},{4,28},{5,29},{6,30},{7,31},{8,0},{9,1... | collective-permute-start | bytes 5013512 | tf_op jit(solution)/shard_map/near/ppermute | solution.py:55
  26.8 0.7 dynamic-slice_bitcast_fusion
  27.5 0.1 broadcast_in_dim.12.experts_ref
  27.5 2.1 %pack_rows.3 = (bf16[2,144,2048]{2,1,0:T(8,128)(2,1)S(1)}, bf16[2,144,2048]{2,1,0:T(8,128)(2,1)S(1)}, bf16[2,144,2048]{2,1,0:T(8,128)(2,1)S(1)}, bf16[2,144,2048]{2,1,0:T(8,128)(2,1)S(1)}) custom-call(s32[8,128]{1,0:T(8,128)S(1)} %broadcast_in_dim.12.experts_ref, bf16[1,128,2176]{2,1,0:T(8,128)(2,1)S(1)} %fusion.2.refs_0_, ...), custom_call_target="tpu_custom_call" | custom-call | flops 603979776 | bytes 7864320 | tf_op jit(solution)/shard_map/pack_rows/pallas_call | solution.py:104
  29.7 1.5 %collective-permute-start.7 = (bf16[2,144,2048]{2,1,0:T(8,128)(2,1)S(1)}, bf16[2,144,2048]{2,1,0:T(8,128)(2,1)S(1)}, u32[]{:S(2)}, u32[]{:S(2)}) collective-permute-start(bf16[2,144,2048]{2,1,0:T(8,128)(2,1)S(1)} %get-tuple-element.54), channel_id=1, source_target_pairs={{0,2},{1,3},{2,0},{3,1},{4,68},{5,69},{6,70},{7,71},{8,10},{9,11},... | collective-permute-start | bytes 3538952 | tf_op jit(solution)/shard_map/F/ppermute | solution.py:55
  31.2 1.1 collective-permute-start.8
  32.3 1.6 %collective-permute-start.9 = (bf16[2,144,2048]{2,1,0:T(8,128)(2,1)S(1)}, bf16[2,144,2048]{2,1,0:T(8,128)(2,1)S(1)}, u32[]{:S(2)}, u32[]{:S(2)}) collective-permute-start(bf16[2,144,2048]{2,1,0:T(8,128)(2,1)S(1)} %get-tuple-element.56), channel_id=1, source_target_pairs={{0,3},{1,0},{2,1},{3,2},{4,100},{5,101},{6,102},{7,103},{8,11},{9,... | collective-permute-start | bytes 3538952 | tf_op jit(solution)/shard_map/F/ppermute | solution.py:55
  33.9 12.8 %collective-permute-done.7.refs_1_ = bf16[2,144,2048]{2,1,0:T(8,128)(2,1)S(1)} collective-permute-done((bf16[2,144,2048]{2,1,0:T(8,128)(2,1)S(1)}, bf16[2,144,2048]{2,1,0:T(8,128)(2,1)S(1)}, u32[]{:S(2)}, u32[]{:S(2)}) %collective-permute-start.7) | collective-permute-done | bytes 1179680 | tf_op jit(solution)/shard_map/F/ppermute | solution.py:55
  46.7 12.6 %collective-permute-done.8.refs_2_ = bf16[2,144,2048]{2,1,0:T(8,128)(2,1)S(1)} collective-permute-done((bf16[2,144,2048]{2,1,0:T(8,128)(2,1)S(1)}, bf16[2,144,2048]{2,1,0:T(8,128)(2,1)S(1)}, u32[]{:S(2)}, u32[]{:S(2)}) %collective-permute-start.8) | collective-permute-done | bytes 1179680 | tf_op jit(solution)/shard_map/F/ppermute | solution.py:55
  59.3 0.0 collective-permute-done.9.refs_3_
  59.3 0.0 copy-done.1
  59.3 5.6 %hidden_gram.6.refs_6_ = f32[776,768]{1,0:T(8,128)S(1)} custom-call(bf16[2,144,2048]{2,1,0:T(8,128)(2,1)S(1)} %get-tuple-element.59.refs_0_, bf16[2,144,2048]{2,1,0:T(8,128)(2,1)S(1)} %collective-permute-done.7.refs_1_, bf16[2,144,2048]{2,1,0:T(8,128)(2,1)S(1)} %collective-permute-done.8.refs_2_, bf16[2,144,2048]{2,1,0:T(8,128)(2,1)S(1)} %collective-permute-done.9.refs_3_, ...), custom_call_target="tpu_custom_call" | custom-call | flops 4303355904 | bytes 13369344 | tf_op jit(solution)/shard_map/hidden_gram/pallas_call | solution.py:162
  64.9 0.0 copy-start.2
  64.9 0.0 collective-permute-done.5.refs_0_
  64.9 0.0 collective-permute-done.6.refs_1_
  64.9 2.8 %collective-permute-start.12 = (bf16[1,2048,768]{2,1,0:T(8,128)(2,1)S(1)}, bf16[1,2048,768]{2,1,0:T(8,128)(2,1)S(1)}, u32[]{:S(2)}, u32[]{:S(2)}) collective-permute-start(bf16[1,2048,768]{2,1,0:T(8,128)(2,1)S(1)} %copy-done), channel_id=1, source_target_pairs={{0,4},{1,5},{2,6},{3,7},{4,0},{5,1},{6,2},{7,3},{8,12},{9,13},{10,... | collective-permute-start | bytes 9437192 | tf_op jit(solution)/shard_map/og/ppermute | solution.py:55
  67.7 0.3 collective-permute-start.13
  68.1 2.2 %pack_rows.4 = (bf16[2,144,2048]{2,1,0:T(8,128)(2,1)S(1)}, bf16[2,144,2048]{2,1,0:T(8,128)(2,1)S(1)}, bf16[2,144,2048]{2,1,0:T(8,128)(2,1)S(1)}, bf16[2,144,2048]{2,1,0:T(8,128)(2,1)S(1)}) custom-call(s32[8,128]{1,0:T(8,128)S(1)} %broadcast_in_dim.12.experts_ref, bf16[3,128,2176]{2,1,0:T(8,128)(2,1)S(1)} %collective-permute-done.5.refs_0_, ...), custom_call_target="tpu_custom_call" | custom-call | flops 603979776 | bytes 7864320 | tf_op jit(solution)/shard_map/pack_rows/pallas_call | solution.py:104
  70.3 0.6 collective-permute-start.14
  70.8 0.3 collective-permute-start.15
  71.2 2.4 %collective-permute-start.16 = (bf16[2,144,2048]{2,1,0:T(8,128)(2,1)S(1)}, bf16[2,144,2048]{2,1,0:T(8,128)(2,1)S(1)}, u32[]{:S(2)}, u32[]{:S(2)}) collective-permute-start(bf16[2,144,2048]{2,1,0:T(8,128)(2,1)S(1)} %get-tuple-element.68), channel_id=1, source_target_pairs={{0,3},{1,0},{2,1},{3,2},{4,100},{5,101},{6,102},{7,103},{8,11},{9,... | collective-permute-start | bytes 3538952 | tf_op jit(solution)/shard_map/F/ppermute | solution.py:55
  73.5 0.1 pad_maximum_fusion.1
  73.6 0.1 slice.7
  73.7 0.0 collective-permute-done.12.refs_4_
  73.7 0.2 collective-permute-start.10
  73.9 3.6 %collective-permute-done.13.refs_5_ = bf16[1,2048,768]{2,1,0:T(8,128)(2,1)S(1)} collective-permute-done((bf16[1,2048,768]{2,1,0:T(8,128)(2,1)S(1)}, bf16[1,2048,768]{2,1,0:T(8,128)(2,1)S(1)}, u32[]{:S(2)}, u32[]{:S(2)}) %collective-permute-start.13) | collective-permute-done | bytes 3145760 | tf_op jit(solution)/shard_map/ou/ppermute | solution.py:55
  77.5 1.4 %collective-permute-start.11 = (bf16[2,128,2176]{2,1,0:T(8,128)(2,1)S(1)}, bf16[2,128,2176]{2,1,0:T(8,128)(2,1)S(1)}, u32[]{:S(2)}, u32[]{:S(2)}) collective-permute-start(bf16[2,128,2176]{2,1,0:T(8,128)(2,1)S(1)} %slice.7), channel_id=1, source_target_pairs={{0,24},{1,25},{2,26},{3,27},{4,28},{5,29},{6,30},{7,31},{8,0},{9,1... | collective-permute-start | bytes 3342344 | tf_op jit(solution)/shard_map/far/ppermute | solution.py:55
  79.0 5.6 %hidden_gram.7.refs_6_ = f32[776,768]{1,0:T(8,128)S(1)} custom-call(bf16[2,144,2048]{2,1,0:T(8,128)(2,1)S(1)} %get-tuple-element.59.refs_0_, bf16[2,144,2048]{2,1,0:T(8,128)(2,1)S(1)} %collective-permute-done.7.refs_1_, bf16[2,144,2048]{2,1,0:T(8,128)(2,1)S(1)} %collective-permute-done.8.refs_2_, bf16[2,144,2048]{2,1,0:T(8,128)(2,1)S(1)} %collective-permute-done.9.refs_3_, ...), custom_call_target="tpu_custom_call" | custom-call | flops 4303355904 | bytes 13369344 | tf_op jit(solution)/shard_map/hidden_gram/pallas_call | solution.py:162
  84.5 15.7 %collective-permute-done.10.refs_0_ = bf16[2,128,2176]{2,1,0:T(8,128)(2,1)S(1)} collective-permute-done((bf16[2,128,2176]{2,1,0:T(8,128)(2,1)S(1)}, bf16[2,128,2176]{2,1,0:T(8,128)(2,1)S(1)}, u32[]{:S(2)}, u32[]{:S(2)}) %collective-permute-start.10) | collective-permute-done | bytes 1114144 | tf_op jit(solution)/shard_map/far/ppermute | solution.py:55
  100.2 3.1 %collective-permute-done.11.refs_1_ = bf16[2,128,2176]{2,1,0:T(8,128)(2,1)S(1)} collective-permute-done((bf16[2,128,2176]{2,1,0:T(8,128)(2,1)S(1)}, bf16[2,128,2176]{2,1,0:T(8,128)(2,1)S(1)}, u32[]{:S(2)}, u32[]{:S(2)}) %collective-permute-start.11) | collective-permute-done | bytes 1114144 | tf_op jit(solution)/shard_map/far/ppermute | solution.py:55
  103.3 0.0 collective-permute-done.14.refs_1_
  103.3 0.0 collective-permute-done.15.refs_2_
  103.3 0.0 collective-permute-done.16.refs_3_
  103.3 1.5 %pack_rows.5 = (bf16[2,96,2048]{2,1,0:T(8,128)(2,1)S(1)}, bf16[2,96,2048]{2,1,0:T(8,128)(2,1)S(1)}, bf16[2,96,2048]{2,1,0:T(8,128)(2,1)S(1)}, bf16[2,96,2048]{2,1,0:T(8,128)(2,1)S(1)}) custom-call(s32[8,128]{1,0:T(8,128)S(1)} %broadcast_in_dim.12.experts_ref, bf16[2,128,2176]{2,1,0:T(8,128)(2,1)S(1)} %collective-permute-done.10.refs_0_, ...), custom_call_target="tpu_custom_call" | custom-call | flops 402653184 | bytes 5242880 | tf_op jit(solution)/shard_map/pack_rows/pallas_call | solution.py:104
  104.8 0.6 collective-permute-start.17
  105.4 0.3 collective-permute-start.18
  105.7 2.4 %collective-permute-start.19 = (bf16[2,96,2048]{2,1,0:T(8,128)(2,1)S(1)}, bf16[2,96,2048]{2,1,0:T(8,128)(2,1)S(1)}, u32[]{:S(2)}, u32[]{:S(2)}) collective-permute-start(bf16[2,96,2048]{2,1,0:T(8,128)(2,1)S(1)} %get-tuple-element.80), channel_id=1, source_target_pairs={{0,3},{1,0},{2,1},{3,2},{4,100},{5,101},{6,102},{7,103},{8,11},{9,... | collective-permute-start | bytes 2359304 | tf_op jit(solution)/shard_map/F/ppermute | solution.py:55
  108.1 1.7 %copy-done.3 = f32[776,768]{1,0:T(8,128)S(1)} copy-done((f32[776,768]{1,0:T(8,128)S(1)}, f32[776,768]{1,0:T(8,128)}, u32[]{:S(2)}) %copy-start.3) | copy-done | bytes 2383896
  109.8 5.6 %hidden_gram.8.refs_6_ = f32[776,768]{1,0:T(8,128)S(1)} custom-call(bf16[2,144,2048]{2,1,0:T(8,128)(2,1)S(1)} %get-tuple-element.69.refs_0_, bf16[2,144,2048]{2,1,0:T(8,128)(2,1)S(1)} %collective-permute-done.14.refs_1_, bf16[2,144,2048]{2,1,0:T(8,128)(2,1)S(1)} %collective-permute-done.15.refs_2_, ...), custom_call_target="tpu_custom_call" | custom-call | flops 4303355904 | bytes 13369344 | tf_op jit(solution)/shard_map/hidden_gram/pallas_call | solution.py:162
  115.4 5.6 %hidden_gram.9.refs_6_ = f32[776,768]{1,0:T(8,128)S(1)} custom-call(bf16[2,144,2048]{2,1,0:T(8,128)(2,1)S(1)} %get-tuple-element.69.refs_0_, bf16[2,144,2048]{2,1,0:T(8,128)(2,1)S(1)} %collective-permute-done.14.refs_1_, bf16[2,144,2048]{2,1,0:T(8,128)(2,1)S(1)} %collective-permute-done.15.refs_2_, ...), custom_call_target="tpu_custom_call" | custom-call | flops 4303355904 | bytes 13369344 | tf_op jit(solution)/shard_map/hidden_gram/pallas_call | solution.py:162
  121.0 0.0 collective-permute-done.17.refs_1_
  121.0 5.0 %collective-permute-done.18.refs_2_ = bf16[2,96,2048]{2,1,0:T(8,128)(2,1)S(1)} collective-permute-done((bf16[2,96,2048]{2,1,0:T(8,128)(2,1)S(1)}, bf16[2,96,2048]{2,1,0:T(8,128)(2,1)S(1)}, u32[]{:S(2)}, u32[]{:S(2)}) %collective-permute-start.18) | collective-permute-done | bytes 786464 | tf_op jit(solution)/shard_map/F/ppermute | solution.py:55
  126.0 0.0 collective-permute-done.19.refs_3_
  126.0 5.5 %hidden_gram.11 = f32[776,768]{1,0:T(8,128)} custom-call(bf16[2,96,2048]{2,1,0:T(8,128)(2,1)S(1)} %get-tuple-element.81.refs_0_, bf16[2,96,2048]{2,1,0:T(8,128)(2,1)S(1)} %collective-permute-done.17.refs_1_, bf16[2,96,2048]{2,1,0:T(8,128)(2,1)S(1)} %collective-permute-done.18.refs_2_, bf16[2,96,2048]{2,1,0:T(8,128)(2,1)S(1)} %collective-permute-done.19.refs_3_, ...), custom_call_target="tpu_custom_call" | custom-call | flops 2868903936 | bytes 12582912 | tf_op jit(solution)/shard_map/hidden_gram/pallas_call | solution.py:162
  131.5 0.0 slice-start.1
  131.5 2.4 %collective-permute-start.20 = (f32[776,768]{1,0:T(8,128)}, f32[776,768]{1,0:T(8,128)S(1)}, u32[]{:S(2)}, u32[]{:S(2)}) collective-permute-start(f32[776,768]{1,0:T(8,128)} %hidden_gram.11), channel_id=1, source_target_pairs={{0,4},{1,5},{2,6},{3,7},{4,0},{5,1},{6,2},{7,3},{8,12},{9,13},{10,... | collective-permute-start | bytes 7151624 | tf_op jit(solution)/shard_map/sums/ppermute | solution.py:55
  133.9 4.1 %hidden_gram.10.one_ref = f32[776,768]{1,0:T(8,128)S(1)} custom-call(bf16[2,96,2048]{2,1,0:T(8,128)(2,1)S(1)} %get-tuple-element.81.refs_0_, bf16[2,96,2048]{2,1,0:T(8,128)(2,1)S(1)} %collective-permute-done.17.refs_1_, bf16[2,96,2048]{2,1,0:T(8,128)(2,1)S(1)} %collective-permute-done.18.refs_2_, bf16[2,96,2048]{2,1,0:T(8,128)(2,1)S(1)} %collective-permute-done.19.refs_3_, ...), custom_call_target="tpu_custom_call" | custom-call | flops 2868903936 | bytes 12582912 | tf_op jit(solution)/shard_map/hidden_gram/pallas_call | solution.py:162
  138.0 0.3 collective-permute-done.20.two_ref
  138.3 0.0 slice-done
  138.3 5.5 %mean_product.1 = f32[1,768,2048]{2,1,0:T(8,128)} custom-call(f32[776,768]{1,0:T(8,128)S(1)} %hidden_gram.10.one_ref, f32[776,768]{1,0:T(8,128)S(1)} %collective-permute-done.20.two_ref, f32[1,768,2048]{2,1,0:T(8,128)S(1)} %bitcast.7), custom_call_target="tpu_custom_call" | custom-call | tf_op jit(solution)/shard_map/mean_product/pallas_call | solution.py:199
  (9 shorter events, 0.1 us)
Async XLA Ops:
  1.8 11.8 %collective-permute-start = (bf16[1,128,2176]{2,1,0:T(8,128)(2,1)S(1)}, bf16[1,128,2176]{2,1,0:T(8,128)(2,1)S(1)}, u32[]{:S(2)}, u32[]{:S(2)}) collective-permute-start(bf16[1,128,2176]{2,1,0:T(8,128)(2,1)S(1)} %fusion.2.refs_0_), channel_id=1, source_target_pairs={{0,64},{1,65},{2,66},{3,67},{4,6},{5,7},{6,4},{7,5},{8,72},{9,73},... | collective-permute-start | bytes 1671176 | tf_op jit(solution)/shard_map/ring/ppermute | solution.py:55
  6.3 13.2 %collective-permute-start.1 = (bf16[1,128,2176]{2,1,0:T(8,128)(2,1)S(1)}, bf16[1,128,2176]{2,1,0:T(8,128)(2,1)S(1)}, u32[]{:S(2)}, u32[]{:S(2)}) collective-permute-start(bf16[1,128,2176]{2,1,0:T(8,128)(2,1)S(1)} %fusion.2.refs_0_), channel_id=1, source_target_pairs={{0,32},{1,33},{2,34},{3,35},{4,5},{5,6},{6,7},{7,4},{8,40},{9,41},... | collective-permute-start | bytes 1671176 | tf_op jit(solution)/shard_map/ring/ppermute | solution.py:55
  7.0 13.2 %collective-permute-start.2 = (bf16[1,128,2176]{2,1,0:T(8,128)(2,1)S(1)}, bf16[1,128,2176]{2,1,0:T(8,128)(2,1)S(1)}, u32[]{:S(2)}, u32[]{:S(2)}) collective-permute-start(bf16[1,128,2176]{2,1,0:T(8,128)(2,1)S(1)} %fusion.2.refs_0_), channel_id=1, source_target_pairs={{0,96},{1,97},{2,98},{3,99},{4,7},{5,4},{6,5},{7,6},{8,104},{9,105... | collective-permute-start | bytes 1671176 | tf_op jit(solution)/shard_map/ring/ppermute | solution.py:55
  9.0 14.8 %collective-permute-start.3 = (bf16[1,128,2176]{2,1,0:T(8,128)(2,1)S(1)}, bf16[1,128,2176]{2,1,0:T(8,128)(2,1)S(1)}, u32[]{:S(2)}, u32[]{:S(2)}) collective-permute-start(bf16[1,128,2176]{2,1,0:T(8,128)(2,1)S(1)} %fusion.2.refs_0_), channel_id=1, source_target_pairs={{0,8},{1,9},{2,10},{3,11},{4,12},{5,13},{6,14},{7,15},{8,16},{9,17... | collective-permute-start | bytes 1671176 | tf_op jit(solution)/shard_map/own/ppermute | solution.py:55
  10.3 13.6 %collective-permute-start.4 = (bf16[1,128,2176]{2,1,0:T(8,128)(2,1)S(1)}, bf16[1,128,2176]{2,1,0:T(8,128)(2,1)S(1)}, u32[]{:S(2)}, u32[]{:S(2)}) collective-permute-start(bf16[1,128,2176]{2,1,0:T(8,128)(2,1)S(1)} %fusion.2.refs_0_), channel_id=1, source_target_pairs={{0,24},{1,25},{2,26},{3,27},{4,28},{5,29},{6,30},{7,31},{8,0},{9,1... | collective-permute-start | bytes 1671176 | tf_op jit(solution)/shard_map/own/ppermute | solution.py:55
  23.8 35.5 %copy-start.1 = (bf16[1,2048,768]{2,1,0:T(8,128)(2,1)S(1)}, bf16[1,2048,768]{2,1,0:T(8,128)(2,1)}, u32[]{:S(2)}) copy-start(bf16[1,2048,768]{2,1,0:T(8,128)(2,1)} %refs_5_.5) | copy-start | bytes 9437188
  24.0 40.9 %collective-permute-start.5 = (bf16[3,128,2176]{2,1,0:T(8,128)(2,1)S(1)}, bf16[3,128,2176]{2,1,0:T(8,128)(2,1)S(1)}, u32[]{:S(2)}, u32[]{:S(2)}) collective-permute-start(bf16[3,128,2176]{2,1,0:T(8,128)(2,1)S(1)} %pad_maximum_fusion), channel_id=1, source_target_pairs={{0,8},{1,9},{2,10},{3,11},{4,12},{5,13},{6,14},{7,15},{8,16},{9,17... | collective-permute-start | bytes 5013512 | tf_op jit(solution)/shard_map/near/ppermute | solution.py:55
  25.0 39.9 %collective-permute-start.6 = (bf16[3,128,2176]{2,1,0:T(8,128)(2,1)S(1)}, bf16[3,128,2176]{2,1,0:T(8,128)(2,1)S(1)}, u32[]{:S(2)}, u32[]{:S(2)}) collective-permute-start(bf16[3,128,2176]{2,1,0:T(8,128)(2,1)S(1)} %pad_maximum_fusion), channel_id=1, source_target_pairs={{0,24},{1,25},{2,26},{3,27},{4,28},{5,29},{6,30},{7,31},{8,0},{9,1... | collective-permute-start | bytes 5013512 | tf_op jit(solution)/shard_map/near/ppermute | solution.py:55
  27.5 31.7 %copy-start = (bf16[1,2048,768]{2,1,0:T(8,128)(2,1)S(1)}, bf16[1,2048,768]{2,1,0:T(8,128)(2,1)}, u32[]{:S(2)}) copy-start(bf16[1,2048,768]{2,1,0:T(8,128)(2,1)} %refs_4_.5) | copy-start | bytes 9437188
  29.7 17.0 %collective-permute-start.7 = (bf16[2,144,2048]{2,1,0:T(8,128)(2,1)S(1)}, bf16[2,144,2048]{2,1,0:T(8,128)(2,1)S(1)}, u32[]{:S(2)}, u32[]{:S(2)}) collective-permute-start(bf16[2,144,2048]{2,1,0:T(8,128)(2,1)S(1)} %get-tuple-element.54), channel_id=1, source_target_pairs={{0,2},{1,3},{2,0},{3,1},{4,68},{5,69},{6,70},{7,71},{8,10},{9,11},... | collective-permute-start | bytes 3538952 | tf_op jit(solution)/shard_map/F/ppermute | solution.py:55
  31.2 28.1 %collective-permute-start.8 = (bf16[2,144,2048]{2,1,0:T(8,128)(2,1)S(1)}, bf16[2,144,2048]{2,1,0:T(8,128)(2,1)S(1)}, u32[]{:S(2)}, u32[]{:S(2)}) collective-permute-start(bf16[2,144,2048]{2,1,0:T(8,128)(2,1)S(1)} %get-tuple-element.55), channel_id=1, source_target_pairs={{0,1},{1,2},{2,3},{3,0},{4,36},{5,37},{6,38},{7,39},{8,9},{9,10},{... | collective-permute-start | bytes 3538952 | tf_op jit(solution)/shard_map/F/ppermute | solution.py:55
  32.3 27.0 %collective-permute-start.9 = (bf16[2,144,2048]{2,1,0:T(8,128)(2,1)S(1)}, bf16[2,144,2048]{2,1,0:T(8,128)(2,1)S(1)}, u32[]{:S(2)}, u32[]{:S(2)}) collective-permute-start(bf16[2,144,2048]{2,1,0:T(8,128)(2,1)S(1)} %get-tuple-element.56), channel_id=1, source_target_pairs={{0,3},{1,0},{2,1},{3,2},{4,100},{5,101},{6,102},{7,103},{8,11},{9,... | collective-permute-start | bytes 3538952 | tf_op jit(solution)/shard_map/F/ppermute | solution.py:55
  64.9 5.4 %copy-start.2 = (f32[776,768]{1,0:T(8,128)}, f32[776,768]{1,0:T(8,128)S(1)}, u32[]{:S(2)}) copy-start(f32[776,768]{1,0:T(8,128)S(1)} %hidden_gram.6.refs_6_) | copy-start | bytes 7151620
  64.9 8.8 %collective-permute-start.12 = (bf16[1,2048,768]{2,1,0:T(8,128)(2,1)S(1)}, bf16[1,2048,768]{2,1,0:T(8,128)(2,1)S(1)}, u32[]{:S(2)}, u32[]{:S(2)}) collective-permute-start(bf16[1,2048,768]{2,1,0:T(8,128)(2,1)S(1)} %copy-done), channel_id=1, source_target_pairs={{0,4},{1,5},{2,6},{3,7},{4,0},{5,1},{6,2},{7,3},{8,12},{9,13},{10,... | collective-permute-start | bytes 9437192 | tf_op jit(solution)/shard_map/og/ppermute | solution.py:55
  67.7 9.8 %collective-permute-start.13 = (bf16[1,2048,768]{2,1,0:T(8,128)(2,1)S(1)}, bf16[1,2048,768]{2,1,0:T(8,128)(2,1)S(1)}, u32[]{:S(2)}, u32[]{:S(2)}) collective-permute-start(bf16[1,2048,768]{2,1,0:T(8,128)(2,1)S(1)} %copy-done.1), channel_id=1, source_target_pairs={{0,4},{1,5},{2,6},{3,7},{4,0},{5,1},{6,2},{7,3},{8,12},{9,13},{10,... | collective-permute-start | bytes 9437192 | tf_op jit(solution)/shard_map/ou/ppermute | solution.py:55
  70.3 33.0 %collective-permute-start.14 = (bf16[2,144,2048]{2,1,0:T(8,128)(2,1)S(1)}, bf16[2,144,2048]{2,1,0:T(8,128)(2,1)S(1)}, u32[]{:S(2)}, u32[]{:S(2)}) collective-permute-start(bf16[2,144,2048]{2,1,0:T(8,128)(2,1)S(1)} %get-tuple-element.66), channel_id=1, source_target_pairs={{0,2},{1,3},{2,0},{3,1},{4,68},{5,69},{6,70},{7,71},{8,10},{9,11},... | collective-permute-start | bytes 3538952 | tf_op jit(solution)/shard_map/F/ppermute | solution.py:55
  70.8 32.5 %collective-permute-start.15 = (bf16[2,144,2048]{2,1,0:T(8,128)(2,1)S(1)}, bf16[2,144,2048]{2,1,0:T(8,128)(2,1)S(1)}, u32[]{:S(2)}, u32[]{:S(2)}) collective-permute-start(bf16[2,144,2048]{2,1,0:T(8,128)(2,1)S(1)} %get-tuple-element.67), channel_id=1, source_target_pairs={{0,1},{1,2},{2,3},{3,0},{4,36},{5,37},{6,38},{7,39},{8,9},{9,10},{... | collective-permute-start | bytes 3538952 | tf_op jit(solution)/shard_map/F/ppermute | solution.py:55
  71.2 32.2 %collective-permute-start.16 = (bf16[2,144,2048]{2,1,0:T(8,128)(2,1)S(1)}, bf16[2,144,2048]{2,1,0:T(8,128)(2,1)S(1)}, u32[]{:S(2)}, u32[]{:S(2)}) collective-permute-start(bf16[2,144,2048]{2,1,0:T(8,128)(2,1)S(1)} %get-tuple-element.68), channel_id=1, source_target_pairs={{0,3},{1,0},{2,1},{3,2},{4,100},{5,101},{6,102},{7,103},{8,11},{9,... | collective-permute-start | bytes 3538952 | tf_op jit(solution)/shard_map/F/ppermute | solution.py:55
  73.7 26.5 %collective-permute-start.10 = (bf16[2,128,2176]{2,1,0:T(8,128)(2,1)S(1)}, bf16[2,128,2176]{2,1,0:T(8,128)(2,1)S(1)}, u32[]{:S(2)}, u32[]{:S(2)}) collective-permute-start(bf16[2,128,2176]{2,1,0:T(8,128)(2,1)S(1)} %pad_maximum_fusion.1), channel_id=1, source_target_pairs={{0,8},{1,9},{2,10},{3,11},{4,12},{5,13},{6,14},{7,15},{8,16},{9,17... | collective-permute-start | bytes 3342344 | tf_op jit(solution)/shard_map/far/ppermute | solution.py:55
  77.5 25.8 %collective-permute-start.11 = (bf16[2,128,2176]{2,1,0:T(8,128)(2,1)S(1)}, bf16[2,128,2176]{2,1,0:T(8,128)(2,1)S(1)}, u32[]{:S(2)}, u32[]{:S(2)}) collective-permute-start(bf16[2,128,2176]{2,1,0:T(8,128)(2,1)S(1)} %slice.7), channel_id=1, source_target_pairs={{0,24},{1,25},{2,26},{3,27},{4,28},{5,29},{6,30},{7,31},{8,0},{9,1... | collective-permute-start | bytes 3342344 | tf_op jit(solution)/shard_map/far/ppermute | solution.py:55
  104.8 16.1 %collective-permute-start.17 = (bf16[2,96,2048]{2,1,0:T(8,128)(2,1)S(1)}, bf16[2,96,2048]{2,1,0:T(8,128)(2,1)S(1)}, u32[]{:S(2)}, u32[]{:S(2)}) collective-permute-start(bf16[2,96,2048]{2,1,0:T(8,128)(2,1)S(1)} %get-tuple-element.78), channel_id=1, source_target_pairs={{0,2},{1,3},{2,0},{3,1},{4,68},{5,69},{6,70},{7,71},{8,10},{9,11},... | collective-permute-start | bytes 2359304 | tf_op jit(solution)/shard_map/F/ppermute | solution.py:55
  105.4 20.6 %collective-permute-start.18 = (bf16[2,96,2048]{2,1,0:T(8,128)(2,1)S(1)}, bf16[2,96,2048]{2,1,0:T(8,128)(2,1)S(1)}, u32[]{:S(2)}, u32[]{:S(2)}) collective-permute-start(bf16[2,96,2048]{2,1,0:T(8,128)(2,1)S(1)} %get-tuple-element.79), channel_id=1, source_target_pairs={{0,1},{1,2},{2,3},{3,0},{4,36},{5,37},{6,38},{7,39},{8,9},{9,10},{... | collective-permute-start | bytes 2359304 | tf_op jit(solution)/shard_map/F/ppermute | solution.py:55
  105.7 20.2 %collective-permute-start.19 = (bf16[2,96,2048]{2,1,0:T(8,128)(2,1)S(1)}, bf16[2,96,2048]{2,1,0:T(8,128)(2,1)S(1)}, u32[]{:S(2)}, u32[]{:S(2)}) collective-permute-start(bf16[2,96,2048]{2,1,0:T(8,128)(2,1)S(1)} %get-tuple-element.80), channel_id=1, source_target_pairs={{0,3},{1,0},{2,1},{3,2},{4,100},{5,101},{6,102},{7,103},{8,11},{9,... | collective-permute-start | bytes 2359304 | tf_op jit(solution)/shard_map/F/ppermute | solution.py:55
  108.1 1.7 %copy-start.3 = (f32[776,768]{1,0:T(8,128)S(1)}, f32[776,768]{1,0:T(8,128)}, u32[]{:S(2)}) copy-start(f32[776,768]{1,0:T(8,128)} %copy-done.2) | copy-start | bytes 7151620
  126.0 12.3 %slice-start = ((s8[6291456]{0:T(1024)(128)(4,1)}), s8[4194304]{0:T(1024)(128)(4,1)S(1)}, s32[]{:S(2)}) async-start(s8[6291456]{0:T(1024)(128)(4,1)} %bitcast.6), calls=%async_computation | async-start | bytes 8388608
  131.5 6.8 %slice-start.1 = ((s8[6291456]{0:T(1024)(128)(4,1)}), s8[2097152]{0:T(1024)(128)(4,1)S(1)}, s32[]{:S(2)}) async-start(s8[6291456]{0:T(1024)(128)(4,1)} %bitcast.6), calls=%async_computation.1 | async-start | bytes 4194304
  131.5 6.8 %collective-permute-start.20 = (f32[776,768]{1,0:T(8,128)}, f32[776,768]{1,0:T(8,128)S(1)}, u32[]{:S(2)}, u32[]{:S(2)}) collective-permute-start(f32[776,768]{1,0:T(8,128)} %hidden_gram.11), channel_id=1, source_target_pairs={{0,4},{1,5},{2,6},{3,7},{4,0},{5,1},{6,2},{7,3},{8,12},{9,13},{10,... | collective-permute-start | bytes 7151624 | tf_op jit(solution)/shard_map/sums/ppermute | solution.py:55
where the time goes:
time: 144 us
  waiting for transfers between devices  65.2 us (45%)
  Pallas kernels  43.4 us (30%)
  starting transfers between devices  30.4 us (21%)
  local copies, waits for them, and re-layouts  2.58 us (2%)
  other arithmetic  2.1 us (1%)
    ppermute x21, waiting for transfers between devices, move(): return lax.ppermute(value, AXES, route)  65.2 us
    pallas_call x6, Pallas kernels, consume(): pl.pallas_call(functools.partial(consume_kernel, which, more), out_shape=...  32 us
    ppermute x21, starting transfers between devices, move(): return lax.ppermute(value, AXES, route)  30.4 us
    pallas_call x3, Pallas kernels, pack(): pl.pallas_call(functools.partial(pack_kernel, slots), out_shape=[shape] *...  5.86 us
    pallas_call x1, Pallas kernels, finish(): pl.pallas_call(finish_kernel, out_shape=jax.ShapeDtypeStruct(down.shape,...  5.52 us
  transfers between devices with their start and end apart: 21, of which 11 were waited for; matrix products, arithmetic and copies ran while one was open for 1% of the time, Pallas kernels for 21%

commit v1 on v0

--- a/solution.py
+++ b/solution.py
@@ -229,7 +229,7 @@
 
     ring = [move(own, gather_ring(shift), "ring") for shift in (2, 1, -1)]
     own_up, own_down = move(own, along_y(1), "own"), move(own, along_y(-1), "own")
-    *ring, own_up, own_down = tie(*ring, own_up, own_down)
+    ring = tie(*ring)
     near = jnp.concatenate(ring, axis=0)
     near, own = tie(near, own)
     near_up, near_down = move(near, along_y(1), "near"), move(near, along_y(-1), "near")

time: 144 us -> 141 us (0.979)
  waiting for transfers between devices: 65.2 us -> 57.5 us
  starting transfers between devices: 30.4 us -> 35 us
    ppermute x21, waiting for transfers between devices: 65.2 us -> 57.5 us  [move(): return lax.ppermute(value, AXES, route)]
    ppermute x21, starting transfers between devices: 30.4 us -> 35 us  [move(): return lax.ppermute(value, AXES, route)]
  transfers between devices with their start and end apart: 21 -> 21, of which waited for: 11 -> 11; matrix products, arithmetic and copies ran while one was open for 1% -> 1% of each run, Pallas kernels for 21% -> 22%
where the time goes in v1:
time: 141 us
  waiting for transfers between devices  57.5 us (41%)
  Pallas kernels  43.3 us (31%)
  starting transfers between devices  35 us (25%)
  local copies, waits for them, and re-layouts  2.58 us (2%)
  other arithmetic  2.1 us (1%)
    ppermute x21, waiting for transfers between devices, move(): return lax.ppermute(value, AXES, route)  57.5 us
    ppermute x21, starting transfers between devices, move(): return lax.ppermute(value, AXES, route)  35 us
    pallas_call x6, Pallas kernels, consume(): pl.pallas_call(functools.partial(consume_kernel, which, more), out_shape=...  32 us
    pallas_call x3, Pallas kernels, pack(): pl.pallas_call(functools.partial(pack_kernel, slots), out_shape=[shape] *...  5.83 us
    pallas_call x1, Pallas kernels, finish(): pl.pallas_call(finish_kernel, out_shape=jax.ShapeDtypeStruct(down.shape,...  5.52 us
  transfers between devices with their start and end apart: 21, of which 11 were waited for; matrix products, arithmetic and copies ran while one was open for 1% of the time, Pallas kernels for 22%

profile of v1, /device:TPU:1, one launch (start us, length us, event | category | flops | bytes accessed | tf_op | source)
XLA Modules:
  0.0 140.7 jit_solution(7838895718774521225)
XLA Ops:
  0.0 0.7 convert_bitcast_fusion
  0.7 1.1 fusion.2.refs_0_
  1.8 4.5 %collective-permute-start.1 = (bf16[1,128,2176]{2,1,0:T(8,128)(2,1)S(1)}, bf16[1,128,2176]{2,1,0:T(8,128)(2,1)S(1)}, u32[]{:S(2)}, u32[]{:S(2)}) collective-permute-start(bf16[1,128,2176]{2,1,0:T(8,128)(2,1)S(1)} %fusion.2.refs_0_), channel_id=1, source_target_pairs={{0,64},{1,65},{2,66},{3,67},{4,6},{5,7},{6,4},{7,5},{8,72},{9,73},... | collective-permute-start | bytes 1671176 | tf_op jit(solution)/shard_map/ring/ppermute | solution.py:55
  6.3 0.7 collective-permute-start.2
  7.0 1.9 %collective-permute-start.3 = (bf16[1,128,2176]{2,1,0:T(8,128)(2,1)S(1)}, bf16[1,128,2176]{2,1,0:T(8,128)(2,1)S(1)}, u32[]{:S(2)}, u32[]{:S(2)}) collective-permute-start(bf16[1,128,2176]{2,1,0:T(8,128)(2,1)S(1)} %fusion.2.refs_0_), channel_id=1, source_target_pairs={{0,96},{1,97},{2,98},{3,99},{4,7},{5,4},{6,5},{7,6},{8,104},{9,105... | collective-permute-start | bytes 1671176 | tf_op jit(solution)/shard_map/ring/ppermute | solution.py:55
  9.0 1.3 collective-permute-start
  10.3 1.4 %collective-permute-start.6 = (bf16[1,128,2176]{2,1,0:T(8,128)(2,1)S(1)}, bf16[1,128,2176]{2,1,0:T(8,128)(2,1)S(1)}, u32[]{:S(2)}, u32[]{:S(2)}) collective-permute-start(bf16[1,128,2176]{2,1,0:T(8,128)(2,1)S(1)} %fusion.2.refs_0_), channel_id=1, source_target_pairs={{0,24},{1,25},{2,26},{3,27},{4,28},{5,29},{6,30},{7,31},{8,0},{9,1... | collective-permute-start | bytes 1671176 | tf_op jit(solution)/shard_map/own/ppermute | solution.py:55
  11.7 1.8 %collective-permute-done.1.refs_1_ = bf16[1,128,2176]{2,1,0:T(8,128)(2,1)S(1)} collective-permute-done((bf16[1,128,2176]{2,1,0:T(8,128)(2,1)S(1)}, bf16[1,128,2176]{2,1,0:T(8,128)(2,1)S(1)}, u32[]{:S(2)}, u32[]{:S(2)}) %collective-permute-start.1) | collective-permute-done | bytes 557088 | tf_op jit(solution)/shard_map/ring/ppermute | solution.py:55
  13.5 5.9 %collective-permute-done.2.refs_2_ = bf16[1,128,2176]{2,1,0:T(8,128)(2,1)S(1)} collective-permute-done((bf16[1,128,2176]{2,1,0:T(8,128)(2,1)S(1)}, bf16[1,128,2176]{2,1,0:T(8,128)(2,1)S(1)}, u32[]{:S(2)}, u32[]{:S(2)}) %collective-permute-start.2) | collective-permute-done | bytes 557088 | tf_op jit(solution)/shard_map/ring/ppermute | solution.py:55
  19.5 0.8 collective-permute-done.3.refs_3_
  20.2 0.2 pad_maximum_fusion
  20.5 1.4 collective-permute-start.4
  21.8 1.5 %collective-permute-start.5 = (bf16[3,128,2176]{2,1,0:T(8,128)(2,1)S(1)}, bf16[3,128,2176]{2,1,0:T(8,128)(2,1)S(1)}, u32[]{:S(2)}, u32[]{:S(2)}) collective-permute-start(bf16[3,128,2176]{2,1,0:T(8,128)(2,1)S(1)} %pad_maximum_fusion), channel_id=1, source_target_pairs={{0,24},{1,25},{2,26},{3,27},{4,28},{5,29},{6,30},{7,31},{8,0},{9,1... | collective-permute-start | bytes 5013512 | tf_op jit(solution)/shard_map/near/ppermute | solution.py:55
  23.4 0.7 dynamic-slice_bitcast_fusion
  24.0 0.0 collective-permute-done.refs_4_
  24.0 0.0 collective-permute-done.6.refs_5_
  24.0 0.1 broadcast_in_dim.12.experts_ref
  24.1 2.2 %pack_rows.3 = (bf16[2,144,2048]{2,1,0:T(8,128)(2,1)S(1)}, bf16[2,144,2048]{2,1,0:T(8,128)(2,1)S(1)}, bf16[2,144,2048]{2,1,0:T(8,128)(2,1)S(1)}, bf16[2,144,2048]{2,1,0:T(8,128)(2,1)S(1)}) custom-call(s32[8,128]{1,0:T(8,128)S(1)} %broadcast_in_dim.12.experts_ref, bf16[1,128,2176]{2,1,0:T(8,128)(2,1)S(1)} %fusion.2.refs_0_, ...), custom_call_target="tpu_custom_call" | custom-call | flops 603979776 | bytes 7864320 | tf_op jit(solution)/shard_map/pack_rows/pallas_call | solution.py:104
  26.3 2.8 %collective-permute-start.7 = (bf16[2,144,2048]{2,1,0:T(8,128)(2,1)S(1)}, bf16[2,144,2048]{2,1,0:T(8,128)(2,1)S(1)}, u32[]{:S(2)}, u32[]{:S(2)}) collective-permute-start(bf16[2,144,2048]{2,1,0:T(8,128)(2,1)S(1)} %get-tuple-element.50), channel_id=1, source_target_pairs={{0,2},{1,3},{2,0},{3,1},{4,68},{5,69},{6,70},{7,71},{8,10},{9,11},... | collective-permute-start | bytes 3538952 | tf_op jit(solution)/shard_map/F/ppermute | solution.py:55
  29.1 0.3 collective-permute-start.8
  29.5 2.4 %collective-permute-start.9 = (bf16[2,144,2048]{2,1,0:T(8,128)(2,1)S(1)}, bf16[2,144,2048]{2,1,0:T(8,128)(2,1)S(1)}, u32[]{:S(2)}, u32[]{:S(2)}) collective-permute-start(bf16[2,144,2048]{2,1,0:T(8,128)(2,1)S(1)} %get-tuple-element.52), channel_id=1, source_target_pairs={{0,3},{1,0},{2,1},{3,2},{4,100},{5,101},{6,102},{7,103},{8,11},{9,... | collective-permute-start | bytes 3538952 | tf_op jit(solution)/shard_map/F/ppermute | solution.py:55
  31.8 11.5 %collective-permute-done.7.refs_1_ = bf16[2,144,2048]{2,1,0:T(8,128)(2,1)S(1)} collective-permute-done((bf16[2,144,2048]{2,1,0:T(8,128)(2,1)S(1)}, bf16[2,144,2048]{2,1,0:T(8,128)(2,1)S(1)}, u32[]{:S(2)}, u32[]{:S(2)}) %collective-permute-start.7) | collective-permute-done | bytes 1179680 | tf_op jit(solution)/shard_map/F/ppermute | solution.py:55
  43.3 12.6 %collective-permute-done.8.refs_2_ = bf16[2,144,2048]{2,1,0:T(8,128)(2,1)S(1)} collective-permute-done((bf16[2,144,2048]{2,1,0:T(8,128)(2,1)S(1)}, bf16[2,144,2048]{2,1,0:T(8,128)(2,1)S(1)}, u32[]{:S(2)}, u32[]{:S(2)}) %collective-permute-start.8) | collective-permute-done | bytes 1179680 | tf_op jit(solution)/shard_map/F/ppermute | solution.py:55
  55.9 0.1 collective-permute-done.9.refs_3_
  56.0 0.0 copy-done.1
  56.0 0.0 copy-done
  56.0 5.6 %hidden_gram.6.refs_6_ = f32[776,768]{1,0:T(8,128)S(1)} custom-call(bf16[2,144,2048]{2,1,0:T(8,128)(2,1)S(1)} %get-tuple-element.55.refs_0_, bf16[2,144,2048]{2,1,0:T(8,128)(2,1)S(1)} %collective-permute-done.7.refs_1_, bf16[2,144,2048]{2,1,0:T(8,128)(2,1)S(1)} %collective-permute-done.8.refs_2_, bf16[2,144,2048]{2,1,0:T(8,128)(2,1)S(1)} %collective-permute-done.9.refs_3_, ...), custom_call_target="tpu_custom_call" | custom-call | flops 4303355904 | bytes 13369344 | tf_op jit(solution)/shard_map/hidden_gram/pallas_call | solution.py:162
  61.6 0.0 copy-start.2
  61.6 0.0 collective-permute-done.4.refs_0_
  61.7 0.0 collective-permute-done.5.refs_1_
  61.7 2.9 %collective-permute-start.12 = (bf16[1,2048,768]{2,1,0:T(8,128)(2,1)S(1)}, bf16[1,2048,768]{2,1,0:T(8,128)(2,1)S(1)}, u32[]{:S(2)}, u32[]{:S(2)}) collective-permute-start(bf16[1,2048,768]{2,1,0:T(8,128)(2,1)S(1)} %copy-done), channel_id=1, source_target_pairs={{0,4},{1,5},{2,6},{3,7},{4,0},{5,1},{6,2},{7,3},{8,12},{9,13},{10,... | collective-permute-start | bytes 9437192 | tf_op jit(solution)/shard_map/og/ppermute | solution.py:55
  64.5 0.3 collective-permute-start.13
  64.9 2.2 %pack_rows.4 = (bf16[2,144,2048]{2,1,0:T(8,128)(2,1)S(1)}, bf16[2,144,2048]{2,1,0:T(8,128)(2,1)S(1)}, bf16[2,144,2048]{2,1,0:T(8,128)(2,1)S(1)}, bf16[2,144,2048]{2,1,0:T(8,128)(2,1)S(1)}) custom-call(s32[8,128]{1,0:T(8,128)S(1)} %broadcast_in_dim.12.experts_ref, bf16[3,128,2176]{2,1,0:T(8,128)(2,1)S(1)} %collective-permute-done.4.refs_0_, ...), custom_call_target="tpu_custom_call" | custom-call | flops 603979776 | bytes 7864320 | tf_op jit(solution)/shard_map/pack_rows/pallas_call | solution.py:104
  67.0 1.8 %collective-permute-start.14 = (bf16[2,144,2048]{2,1,0:T(8,128)(2,1)S(1)}, bf16[2,144,2048]{2,1,0:T(8,128)(2,1)S(1)}, u32[]{:S(2)}, u32[]{:S(2)}) collective-permute-start(bf16[2,144,2048]{2,1,0:T(8,128)(2,1)S(1)} %get-tuple-element.62), channel_id=1, source_target_pairs={{0,2},{1,3},{2,0},{3,1},{4,68},{5,69},{6,70},{7,71},{8,10},{9,11},... | collective-permute-start | bytes 3538952 | tf_op jit(solution)/shard_map/F/ppermute | solution.py:55
  68.8 1.2 collective-permute-start.15
  70.0 1.5 %collective-permute-start.16 = (bf16[2,144,2048]{2,1,0:T(8,128)(2,1)S(1)}, bf16[2,144,2048]{2,1,0:T(8,128)(2,1)S(1)}, u32[]{:S(2)}, u32[]{:S(2)}) collective-permute-start(bf16[2,144,2048]{2,1,0:T(8,128)(2,1)S(1)} %get-tuple-element.64), channel_id=1, source_target_pairs={{0,3},{1,0},{2,1},{3,2},{4,100},{5,101},{6,102},{7,103},{8,11},{9,... | collective-permute-start | bytes 3538952 | tf_op jit(solution)/shard_map/F/ppermute | solution.py:55
  71.5 0.1 pad_maximum_fusion.1
  71.6 0.1 slice.7
  71.7 0.0 collective-permute-done.12.refs_4_
  71.7 0.2 collective-permute-start.10
  71.9 2.4 %collective-permute-done.13.refs_5_ = bf16[1,2048,768]{2,1,0:T(8,128)(2,1)S(1)} collective-permute-done((bf16[1,2048,768]{2,1,0:T(8,128)(2,1)S(1)}, bf16[1,2048,768]{2,1,0:T(8,128)(2,1)S(1)}, u32[]{:S(2)}, u32[]{:S(2)}) %collective-permute-start.13) | collective-permute-done | bytes 3145760 | tf_op jit(solution)/shard_map/ou/ppermute | solution.py:55
  74.3 2.0 %collective-permute-start.11 = (bf16[2,128,2176]{2,1,0:T(8,128)(2,1)S(1)}, bf16[2,128,2176]{2,1,0:T(8,128)(2,1)S(1)}, u32[]{:S(2)}, u32[]{:S(2)}) collective-permute-start(bf16[2,128,2176]{2,1,0:T(8,128)(2,1)S(1)} %slice.7), channel_id=1, source_target_pairs={{0,24},{1,25},{2,26},{3,27},{4,28},{5,29},{6,30},{7,31},{8,0},{9,1... | collective-permute-start | bytes 3342344 | tf_op jit(solution)/shard_map/far/ppermute | solution.py:55
  76.3 5.6 %hidden_gram.7.refs_6_ = f32[776,768]{1,0:T(8,128)S(1)} custom-call(bf16[2,144,2048]{2,1,0:T(8,128)(2,1)S(1)} %get-tuple-element.55.refs_0_, bf16[2,144,2048]{2,1,0:T(8,128)(2,1)S(1)} %collective-permute-done.7.refs_1_, bf16[2,144,2048]{2,1,0:T(8,128)(2,1)S(1)} %collective-permute-done.8.refs_2_, bf16[2,144,2048]{2,1,0:T(8,128)(2,1)S(1)} %collective-permute-done.9.refs_3_, ...), custom_call_target="tpu_custom_call" | custom-call | flops 4303355904 | bytes 13369344 | tf_op jit(solution)/shard_map/hidden_gram/pallas_call | solution.py:162
  81.9 16.0 %collective-permute-done.10.refs_0_ = bf16[2,128,2176]{2,1,0:T(8,128)(2,1)S(1)} collective-permute-done((bf16[2,128,2176]{2,1,0:T(8,128)(2,1)S(1)}, bf16[2,128,2176]{2,1,0:T(8,128)(2,1)S(1)}, u32[]{:S(2)}, u32[]{:S(2)}) %collective-permute-start.10) | collective-permute-done | bytes 1114144 | tf_op jit(solution)/shard_map/far/ppermute | solution.py:55
  97.9 2.2 %collective-permute-done.11.refs_1_ = bf16[2,128,2176]{2,1,0:T(8,128)(2,1)S(1)} collective-permute-done((bf16[2,128,2176]{2,1,0:T(8,128)(2,1)S(1)}, bf16[2,128,2176]{2,1,0:T(8,128)(2,1)S(1)}, u32[]{:S(2)}, u32[]{:S(2)}) %collective-permute-start.11) | collective-permute-done | bytes 1114144 | tf_op jit(solution)/shard_map/far/ppermute | solution.py:55
  100.1 0.0 collective-permute-done.14.refs_1_
  100.1 0.0 collective-permute-done.15.refs_2_
  100.1 0.0 collective-permute-done.16.refs_3_
  100.1 1.5 %pack_rows.5 = (bf16[2,96,2048]{2,1,0:T(8,128)(2,1)S(1)}, bf16[2,96,2048]{2,1,0:T(8,128)(2,1)S(1)}, bf16[2,96,2048]{2,1,0:T(8,128)(2,1)S(1)}, bf16[2,96,2048]{2,1,0:T(8,128)(2,1)S(1)}) custom-call(s32[8,128]{1,0:T(8,128)S(1)} %broadcast_in_dim.12.experts_ref, bf16[2,128,2176]{2,1,0:T(8,128)(2,1)S(1)} %collective-permute-done.10.refs_0_, ...), custom_call_target="tpu_custom_call" | custom-call | flops 402653184 | bytes 5242880 | tf_op jit(solution)/shard_map/pack_rows/pallas_call | solution.py:104
  101.6 1.8 %collective-permute-start.17 = (bf16[2,96,2048]{2,1,0:T(8,128)(2,1)S(1)}, bf16[2,96,2048]{2,1,0:T(8,128)(2,1)S(1)}, u32[]{:S(2)}, u32[]{:S(2)}) collective-permute-start(bf16[2,96,2048]{2,1,0:T(8,128)(2,1)S(1)} %get-tuple-element.74), channel_id=1, source_target_pairs={{0,2},{1,3},{2,0},{3,1},{4,68},{5,69},{6,70},{7,71},{8,10},{9,11},... | collective-permute-start | bytes 2359304 | tf_op jit(solution)/shard_map/F/ppermute | solution.py:55
  103.4 1.2 collective-permute-start.18
  104.6 1.5 %collective-permute-start.19 = (bf16[2,96,2048]{2,1,0:T(8,128)(2,1)S(1)}, bf16[2,96,2048]{2,1,0:T(8,128)(2,1)S(1)}, u32[]{:S(2)}, u32[]{:S(2)}) collective-permute-start(bf16[2,96,2048]{2,1,0:T(8,128)(2,1)S(1)} %get-tuple-element.76), channel_id=1, source_target_pairs={{0,3},{1,0},{2,1},{3,2},{4,100},{5,101},{6,102},{7,103},{8,11},{9,... | collective-permute-start | bytes 2359304 | tf_op jit(solution)/shard_map/F/ppermute | solution.py:55
  106.1 1.7 %copy-done.3 = f32[776,768]{1,0:T(8,128)S(1)} copy-done((f32[776,768]{1,0:T(8,128)S(1)}, f32[776,768]{1,0:T(8,128)}, u32[]{:S(2)}) %copy-start.3) | copy-done | bytes 2383896
  107.7 5.6 %hidden_gram.8.refs_6_ = f32[776,768]{1,0:T(8,128)S(1)} custom-call(bf16[2,144,2048]{2,1,0:T(8,128)(2,1)S(1)} %get-tuple-element.65.refs_0_, bf16[2,144,2048]{2,1,0:T(8,128)(2,1)S(1)} %collective-permute-done.14.refs_1_, bf16[2,144,2048]{2,1,0:T(8,128)(2,1)S(1)} %collective-permute-done.15.refs_2_, ...), custom_call_target="tpu_custom_call" | custom-call | flops 4303355904 | bytes 13369344 | tf_op jit(solution)/shard_map/hidden_gram/pallas_call | solution.py:162
  113.3 5.6 %hidden_gram.9.refs_6_ = f32[776,768]{1,0:T(8,128)S(1)} custom-call(bf16[2,144,2048]{2,1,0:T(8,128)(2,1)S(1)} %get-tuple-element.65.refs_0_, bf16[2,144,2048]{2,1,0:T(8,128)(2,1)S(1)} %collective-permute-done.14.refs_1_, bf16[2,144,2048]{2,1,0:T(8,128)(2,1)S(1)} %collective-permute-done.15.refs_2_, ...), custom_call_target="tpu_custom_call" | custom-call | flops 4303355904 | bytes 13369344 | tf_op jit(solution)/shard_map/hidden_gram/pallas_call | solution.py:162
  118.9 0.0 collective-permute-done.17.refs_1_
  118.9 3.8 %collective-permute-done.18.refs_2_ = bf16[2,96,2048]{2,1,0:T(8,128)(2,1)S(1)} collective-permute-done((bf16[2,96,2048]{2,1,0:T(8,128)(2,1)S(1)}, bf16[2,96,2048]{2,1,0:T(8,128)(2,1)S(1)}, u32[]{:S(2)}, u32[]{:S(2)}) %collective-permute-start.18) | collective-permute-done | bytes 786464 | tf_op jit(solution)/shard_map/F/ppermute | solution.py:55
  122.8 0.0 collective-permute-done.19.refs_3_
  122.8 5.5 %hidden_gram.11 = f32[776,768]{1,0:T(8,128)} custom-call(bf16[2,96,2048]{2,1,0:T(8,128)(2,1)S(1)} %get-tuple-element.77.refs_0_, bf16[2,96,2048]{2,1,0:T(8,128)(2,1)S(1)} %collective-permute-done.17.refs_1_, bf16[2,96,2048]{2,1,0:T(8,128)(2,1)S(1)} %collective-permute-done.18.refs_2_, bf16[2,96,2048]{2,1,0:T(8,128)(2,1)S(1)} %collective-permute-done.19.refs_3_, ...), custom_call_target="tpu_custom_call" | custom-call | flops 2868903936 | bytes 12582912 | tf_op jit(solution)/shard_map/hidden_gram/pallas_call | solution.py:162
  128.3 0.0 slice-start.1
  128.3 2.4 %collective-permute-start.20 = (f32[776,768]{1,0:T(8,128)}, f32[776,768]{1,0:T(8,128)S(1)}, u32[]{:S(2)}, u32[]{:S(2)}) collective-permute-start(f32[776,768]{1,0:T(8,128)} %hidden_gram.11), channel_id=1, source_target_pairs={{0,4},{1,5},{2,6},{3,7},{4,0},{5,1},{6,2},{7,3},{8,12},{9,13},{10,... | collective-permute-start | bytes 7151624 | tf_op jit(solution)/shard_map/sums/ppermute | solution.py:55
  130.7 4.1 %hidden_gram.10.one_ref = f32[776,768]{1,0:T(8,128)S(1)} custom-call(bf16[2,96,2048]{2,1,0:T(8,128)(2,1)S(1)} %get-tuple-element.77.refs_0_, bf16[2,96,2048]{2,1,0:T(8,128)(2,1)S(1)} %collective-permute-done.17.refs_1_, bf16[2,96,2048]{2,1,0:T(8,128)(2,1)S(1)} %collective-permute-done.18.refs_2_, bf16[2,96,2048]{2,1,0:T(8,128)(2,1)S(1)} %collective-permute-done.19.refs_3_, ...), custom_call_target="tpu_custom_call" | custom-call | flops 2868903936 | bytes 12582912 | tf_op jit(solution)/shard_map/hidden_gram/pallas_call | solution.py:162
  134.8 0.3 collective-permute-done.20.two_ref
  135.1 5.5 %mean_product.1 = f32[1,768,2048]{2,1,0:T(8,128)} custom-call(f32[776,768]{1,0:T(8,128)S(1)} %hidden_gram.10.one_ref, f32[776,768]{1,0:T(8,128)S(1)} %collective-permute-done.20.two_ref, f32[1,768,2048]{2,1,0:T(8,128)S(1)} %bitcast.7), custom_call_target="tpu_custom_call" | custom-call | tf_op jit(solution)/shard_map/mean_product/pallas_call | solution.py:199
  (9 shorter events, 0.1 us)
Async XLA Ops:
  1.8 11.8 %collective-permute-start.1 = (bf16[1,128,2176]{2,1,0:T(8,128)(2,1)S(1)}, bf16[1,128,2176]{2,1,0:T(8,128)(2,1)S(1)}, u32[]{:S(2)}, u32[]{:S(2)}) collective-permute-start(bf16[1,128,2176]{2,1,0:T(8,128)(2,1)S(1)} %fusion.2.refs_0_), channel_id=1, source_target_pairs={{0,64},{1,65},{2,66},{3,67},{4,6},{5,7},{6,4},{7,5},{8,72},{9,73},... | collective-permute-start | bytes 1671176 | tf_op jit(solution)/shard_map/ring/ppermute | solution.py:55
  6.3 13.2 %collective-permute-start.2 = (bf16[1,128,2176]{2,1,0:T(8,128)(2,1)S(1)}, bf16[1,128,2176]{2,1,0:T(8,128)(2,1)S(1)}, u32[]{:S(2)}, u32[]{:S(2)}) collective-permute-start(bf16[1,128,2176]{2,1,0:T(8,128)(2,1)S(1)} %fusion.2.refs_0_), channel_id=1, source_target_pairs={{0,32},{1,33},{2,34},{3,35},{4,5},{5,6},{6,7},{7,4},{8,40},{9,41},... | collective-permute-start | bytes 1671176 | tf_op jit(solution)/shard_map/ring/ppermute | solution.py:55
  7.0 13.2 %collective-permute-start.3 = (bf16[1,128,2176]{2,1,0:T(8,128)(2,1)S(1)}, bf16[1,128,2176]{2,1,0:T(8,128)(2,1)S(1)}, u32[]{:S(2)}, u32[]{:S(2)}) collective-permute-start(bf16[1,128,2176]{2,1,0:T(8,128)(2,1)S(1)} %fusion.2.refs_0_), channel_id=1, source_target_pairs={{0,96},{1,97},{2,98},{3,99},{4,7},{5,4},{6,5},{7,6},{8,104},{9,105... | collective-permute-start | bytes 1671176 | tf_op jit(solution)/shard_map/ring/ppermute | solution.py:55
  9.0 15.1 %collective-permute-start = (bf16[1,128,2176]{2,1,0:T(8,128)(2,1)S(1)}, bf16[1,128,2176]{2,1,0:T(8,128)(2,1)S(1)}, u32[]{:S(2)}, u32[]{:S(2)}) collective-permute-start(bf16[1,128,2176]{2,1,0:T(8,128)(2,1)S(1)} %fusion.2.refs_0_), channel_id=1, source_target_pairs={{0,8},{1,9},{2,10},{3,11},{4,12},{5,13},{6,14},{7,15},{8,16},{9,17... | collective-permute-start | bytes 1671176 | tf_op jit(solution)/shard_map/own/ppermute | solution.py:55
  10.3 13.8 %collective-permute-start.6 = (bf16[1,128,2176]{2,1,0:T(8,128)(2,1)S(1)}, bf16[1,128,2176]{2,1,0:T(8,128)(2,1)S(1)}, u32[]{:S(2)}, u32[]{:S(2)}) collective-permute-start(bf16[1,128,2176]{2,1,0:T(8,128)(2,1)S(1)} %fusion.2.refs_0_), channel_id=1, source_target_pairs={{0,24},{1,25},{2,26},{3,27},{4,28},{5,29},{6,30},{7,31},{8,0},{9,1... | collective-permute-start | bytes 1671176 | tf_op jit(solution)/shard_map/own/ppermute | solution.py:55
  20.2 35.8 %copy-start.1 = (bf16[1,2048,768]{2,1,0:T(8,128)(2,1)S(1)}, bf16[1,2048,768]{2,1,0:T(8,128)(2,1)}, u32[]{:S(2)}) copy-start(bf16[1,2048,768]{2,1,0:T(8,128)(2,1)} %refs_5_.5) | copy-start | bytes 9437188
  20.5 41.2 %collective-permute-start.4 = (bf16[3,128,2176]{2,1,0:T(8,128)(2,1)S(1)}, bf16[3,128,2176]{2,1,0:T(8,128)(2,1)S(1)}, u32[]{:S(2)}, u32[]{:S(2)}) collective-permute-start(bf16[3,128,2176]{2,1,0:T(8,128)(2,1)S(1)} %pad_maximum_fusion), channel_id=1, source_target_pairs={{0,8},{1,9},{2,10},{3,11},{4,12},{5,13},{6,14},{7,15},{8,16},{9,17... | collective-permute-start | bytes 5013512 | tf_op jit(solution)/shard_map/near/ppermute | solution.py:55
  21.8 39.8 %collective-permute-start.5 = (bf16[3,128,2176]{2,1,0:T(8,128)(2,1)S(1)}, bf16[3,128,2176]{2,1,0:T(8,128)(2,1)S(1)}, u32[]{:S(2)}, u32[]{:S(2)}) collective-permute-start(bf16[3,128,2176]{2,1,0:T(8,128)(2,1)S(1)} %pad_maximum_fusion), channel_id=1, source_target_pairs={{0,24},{1,25},{2,26},{3,27},{4,28},{5,29},{6,30},{7,31},{8,0},{9,1... | collective-permute-start | bytes 5013512 | tf_op jit(solution)/shard_map/near/ppermute | solution.py:55
  24.1 31.9 %copy-start = (bf16[1,2048,768]{2,1,0:T(8,128)(2,1)S(1)}, bf16[1,2048,768]{2,1,0:T(8,128)(2,1)}, u32[]{:S(2)}) copy-start(bf16[1,2048,768]{2,1,0:T(8,128)(2,1)} %refs_4_.5) | copy-start | bytes 9437188
  26.3 17.0 %collective-permute-start.7 = (bf16[2,144,2048]{2,1,0:T(8,128)(2,1)S(1)}, bf16[2,144,2048]{2,1,0:T(8,128)(2,1)S(1)}, u32[]{:S(2)}, u32[]{:S(2)}) collective-permute-start(bf16[2,144,2048]{2,1,0:T(8,128)(2,1)S(1)} %get-tuple-element.50), channel_id=1, source_target_pairs={{0,2},{1,3},{2,0},{3,1},{4,68},{5,69},{6,70},{7,71},{8,10},{9,11},... | collective-permute-start | bytes 3538952 | tf_op jit(solution)/shard_map/F/ppermute | solution.py:55
  29.1 26.8 %collective-permute-start.8 = (bf16[2,144,2048]{2,1,0:T(8,128)(2,1)S(1)}, bf16[2,144,2048]{2,1,0:T(8,128)(2,1)S(1)}, u32[]{:S(2)}, u32[]{:S(2)}) collective-permute-start(bf16[2,144,2048]{2,1,0:T(8,128)(2,1)S(1)} %get-tuple-element.51), channel_id=1, source_target_pairs={{0,1},{1,2},{2,3},{3,0},{4,36},{5,37},{6,38},{7,39},{8,9},{9,10},{... | collective-permute-start | bytes 3538952 | tf_op jit(solution)/shard_map/F/ppermute | solution.py:55
  29.5 26.6 %collective-permute-start.9 = (bf16[2,144,2048]{2,1,0:T(8,128)(2,1)S(1)}, bf16[2,144,2048]{2,1,0:T(8,128)(2,1)S(1)}, u32[]{:S(2)}, u32[]{:S(2)}) collective-permute-start(bf16[2,144,2048]{2,1,0:T(8,128)(2,1)S(1)} %get-tuple-element.52), channel_id=1, source_target_pairs={{0,3},{1,0},{2,1},{3,2},{4,100},{5,101},{6,102},{7,103},{8,11},{9,... | collective-permute-start | bytes 3538952 | tf_op jit(solution)/shard_map/F/ppermute | solution.py:55
  61.6 5.4 %copy-start.2 = (f32[776,768]{1,0:T(8,128)}, f32[776,768]{1,0:T(8,128)S(1)}, u32[]{:S(2)}) copy-start(f32[776,768]{1,0:T(8,128)S(1)} %hidden_gram.6.refs_6_) | copy-start | bytes 7151620
  61.7 10.0 %collective-permute-start.12 = (bf16[1,2048,768]{2,1,0:T(8,128)(2,1)S(1)}, bf16[1,2048,768]{2,1,0:T(8,128)(2,1)S(1)}, u32[]{:S(2)}, u32[]{:S(2)}) collective-permute-start(bf16[1,2048,768]{2,1,0:T(8,128)(2,1)S(1)} %copy-done), channel_id=1, source_target_pairs={{0,4},{1,5},{2,6},{3,7},{4,0},{5,1},{6,2},{7,3},{8,12},{9,13},{10,... | collective-permute-start | bytes 9437192 | tf_op jit(solution)/shard_map/og/ppermute | solution.py:55
  64.5 9.8 %collective-permute-start.13 = (bf16[1,2048,768]{2,1,0:T(8,128)(2,1)S(1)}, bf16[1,2048,768]{2,1,0:T(8,128)(2,1)S(1)}, u32[]{:S(2)}, u32[]{:S(2)}) collective-permute-start(bf16[1,2048,768]{2,1,0:T(8,128)(2,1)S(1)} %copy-done.1), channel_id=1, source_target_pairs={{0,4},{1,5},{2,6},{3,7},{4,0},{5,1},{6,2},{7,3},{8,12},{9,13},{10,... | collective-permute-start | bytes 9437192 | tf_op jit(solution)/shard_map/ou/ppermute | solution.py:55
  67.0 33.1 %collective-permute-start.14 = (bf16[2,144,2048]{2,1,0:T(8,128)(2,1)S(1)}, bf16[2,144,2048]{2,1,0:T(8,128)(2,1)S(1)}, u32[]{:S(2)}, u32[]{:S(2)}) collective-permute-start(bf16[2,144,2048]{2,1,0:T(8,128)(2,1)S(1)} %get-tuple-element.62), channel_id=1, source_target_pairs={{0,2},{1,3},{2,0},{3,1},{4,68},{5,69},{6,70},{7,71},{8,10},{9,11},... | collective-permute-start | bytes 3538952 | tf_op jit(solution)/shard_map/F/ppermute | solution.py:55
  68.8 31.3 %collective-permute-start.15 = (bf16[2,144,2048]{2,1,0:T(8,128)(2,1)S(1)}, bf16[2,144,2048]{2,1,0:T(8,128)(2,1)S(1)}, u32[]{:S(2)}, u32[]{:S(2)}) collective-permute-start(bf16[2,144,2048]{2,1,0:T(8,128)(2,1)S(1)} %get-tuple-element.63), channel_id=1, source_target_pairs={{0,1},{1,2},{2,3},{3,0},{4,36},{5,37},{6,38},{7,39},{8,9},{9,10},{... | collective-permute-start | bytes 3538952 | tf_op jit(solution)/shard_map/F/ppermute | solution.py:55
  70.0 30.1 %collective-permute-start.16 = (bf16[2,144,2048]{2,1,0:T(8,128)(2,1)S(1)}, bf16[2,144,2048]{2,1,0:T(8,128)(2,1)S(1)}, u32[]{:S(2)}, u32[]{:S(2)}) collective-permute-start(bf16[2,144,2048]{2,1,0:T(8,128)(2,1)S(1)} %get-tuple-element.64), channel_id=1, source_target_pairs={{0,3},{1,0},{2,1},{3,2},{4,100},{5,101},{6,102},{7,103},{8,11},{9,... | collective-permute-start | bytes 3538952 | tf_op jit(solution)/shard_map/F/ppermute | solution.py:55
  71.7 26.2 %collective-permute-start.10 = (bf16[2,128,2176]{2,1,0:T(8,128)(2,1)S(1)}, bf16[2,128,2176]{2,1,0:T(8,128)(2,1)S(1)}, u32[]{:S(2)}, u32[]{:S(2)}) collective-permute-start(bf16[2,128,2176]{2,1,0:T(8,128)(2,1)S(1)} %pad_maximum_fusion.1), channel_id=1, source_target_pairs={{0,8},{1,9},{2,10},{3,11},{4,12},{5,13},{6,14},{7,15},{8,16},{9,17... | collective-permute-start | bytes 3342344 | tf_op jit(solution)/shard_map/far/ppermute | solution.py:55
  74.3 25.8 %collective-permute-start.11 = (bf16[2,128,2176]{2,1,0:T(8,128)(2,1)S(1)}, bf16[2,128,2176]{2,1,0:T(8,128)(2,1)S(1)}, u32[]{:S(2)}, u32[]{:S(2)}) collective-permute-start(bf16[2,128,2176]{2,1,0:T(8,128)(2,1)S(1)} %slice.7), channel_id=1, source_target_pairs={{0,24},{1,25},{2,26},{3,27},{4,28},{5,29},{6,30},{7,31},{8,0},{9,1... | collective-permute-start | bytes 3342344 | tf_op jit(solution)/shard_map/far/ppermute | solution.py:55
  101.6 17.3 %collective-permute-start.17 = (bf16[2,96,2048]{2,1,0:T(8,128)(2,1)S(1)}, bf16[2,96,2048]{2,1,0:T(8,128)(2,1)S(1)}, u32[]{:S(2)}, u32[]{:S(2)}) collective-permute-start(bf16[2,96,2048]{2,1,0:T(8,128)(2,1)S(1)} %get-tuple-element.74), channel_id=1, source_target_pairs={{0,2},{1,3},{2,0},{3,1},{4,68},{5,69},{6,70},{7,71},{8,10},{9,11},... | collective-permute-start | bytes 2359304 | tf_op jit(solution)/shard_map/F/ppermute | solution.py:55
  103.4 19.4 %collective-permute-start.18 = (bf16[2,96,2048]{2,1,0:T(8,128)(2,1)S(1)}, bf16[2,96,2048]{2,1,0:T(8,128)(2,1)S(1)}, u32[]{:S(2)}, u32[]{:S(2)}) collective-permute-start(bf16[2,96,2048]{2,1,0:T(8,128)(2,1)S(1)} %get-tuple-element.75), channel_id=1, source_target_pairs={{0,1},{1,2},{2,3},{3,0},{4,36},{5,37},{6,38},{7,39},{8,9},{9,10},{... | collective-permute-start | bytes 2359304 | tf_op jit(solution)/shard_map/F/ppermute | solution.py:55
  104.6 18.2 %collective-permute-start.19 = (bf16[2,96,2048]{2,1,0:T(8,128)(2,1)S(1)}, bf16[2,96,2048]{2,1,0:T(8,128)(2,1)S(1)}, u32[]{:S(2)}, u32[]{:S(2)}) collective-permute-start(bf16[2,96,2048]{2,1,0:T(8,128)(2,1)S(1)} %get-tuple-element.76), channel_id=1, source_target_pairs={{0,3},{1,0},{2,1},{3,2},{4,100},{5,101},{6,102},{7,103},{8,11},{9,... | collective-permute-start | bytes 2359304 | tf_op jit(solution)/shard_map/F/ppermute | solution.py:55
  106.1 1.7 %copy-start.3 = (f32[776,768]{1,0:T(8,128)S(1)}, f32[776,768]{1,0:T(8,128)}, u32[]{:S(2)}) copy-start(f32[776,768]{1,0:T(8,128)} %copy-done.2) | copy-start | bytes 7151620
  122.8 12.4 %slice-start = ((s8[6291456]{0:T(1024)(128)(4,1)}), s8[4194304]{0:T(1024)(128)(4,1)S(1)}, s32[]{:S(2)}) async-start(s8[6291456]{0:T(1024)(128)(4,1)} %bitcast.6), calls=%async_computation | async-start | bytes 8388608
  128.3 6.9 %slice-start.1 = ((s8[6291456]{0:T(1024)(128)(4,1)}), s8[2097152]{0:T(1024)(128)(4,1)S(1)}, s32[]{:S(2)}) async-start(s8[6291456]{0:T(1024)(128)(4,1)} %bitcast.6), calls=%async_computation.1 | async-start | bytes 4194304
  128.3 6.8 %collective-permute-start.20 = (f32[776,768]{1,0:T(8,128)}, f32[776,768]{1,0:T(8,128)S(1)}, u32[]{:S(2)}, u32[]{:S(2)}) collective-permute-start(f32[776,768]{1,0:T(8,128)} %hidden_gram.11), channel_id=1, source_target_pairs={{0,4},{1,5},{2,6},{3,7},{4,0},{5,1},{6,2},{7,3},{8,12},{9,13},{10,... | collective-permute-start | bytes 7151624 | tf_op jit(solution)/shard_map/sums/ppermute | solution.py:55

commit v2 on v1

--- a/solution.py
+++ b/solution.py
@@ -106,7 +106,7 @@
         out_shape=[shape] * RING,
         in_specs=[pl.BlockSpec(memory_space=pltpu.VMEM)] * (1 + len(parts)),
         out_specs=[pl.BlockSpec(memory_space=pltpu.VMEM)] * RING,
-        compiler_params=pltpu.CompilerParams(vmem_limit_bytes=24 << 20),
+        compiler_params=pltpu.CompilerParams(vmem_limit_bytes=18 << 20),
         cost_estimate=pl.CostEstimate(
             flops=2 * rows * tokens * width,
             transcendentals=0,
@@ -169,7 +169,7 @@
             pltpu.VMEM((total, width), jnp.bfloat16),
             pltpu.VMEM((total, ff), jnp.bfloat16),
         ],
-        compiler_params=pltpu.CompilerParams(vmem_limit_bytes=28 << 20),
+        compiler_params=pltpu.CompilerParams(vmem_limit_bytes=18 << 20),
         cost_estimate=pl.CostEstimate(
             flops=4 * total * width * ff + 2 * total * ff * ff,
             transcendentals=total * ff,
@@ -203,7 +203,7 @@
         in_specs=[whole, whole, part],
         out_specs=part,
         scratch_shapes=[pltpu.VMEM((ff, ff), jnp.bfloat16)],
-        compiler_params=pltpu.CompilerParams(vmem_limit_bytes=28 << 20),
+        compiler_params=pltpu.CompilerParams(vmem_limit_bytes=18 << 20),
         name="mean_product",
     )(one, two, down)
 

time: 141 us -> 139 us (0.986)
  local copies, waits for them, and re-layouts: 2.58 us -> 0.9 us
    unnamed x12 -> x8, local copies, waits for them, and re-layouts: 1.7 us -> 0.02 us
where the time goes in v2:
time: 139 us
  waiting for transfers between devices  58.9 us (42%)
  Pallas kernels  42 us (30%)
  starting transfers between devices  34.9 us (25%)
  other arithmetic  2.1 us (2%)
    ppermute x21, waiting for transfers between devices, move(): return lax.ppermute(value, AXES, route)  58.9 us
    ppermute x21, starting transfers between devices, move(): return lax.ppermute(value, AXES, route)  34.9 us
    pallas_call x6, Pallas kernels, consume(): pl.pallas_call(functools.partial(consume_kernel, which, more), out_shape=...  30.6 us
    pallas_call x3, Pallas kernels, pack(): pl.pallas_call(functools.partial(pack_kernel, slots), out_shape=[shape] *...  5.91 us
    pallas_call x1, Pallas kernels, finish(): pl.pallas_call(finish_kernel, out_shape=jax.ShapeDtypeStruct(down.shape,...  5.52 us
  transfers between devices with their start and end apart: 21, of which 11 were waited for; matrix products, arithmetic and copies ran while one was open for 1% of the time, Pallas kernels for 22%

profile of v2, /device:TPU:1, one launch (start us, length us, event | category | flops | bytes accessed | tf_op | source)
XLA Modules:
  0.0 139.0 jit_solution(16610695304848877488)
XLA Ops:
  0.0 0.7 convert_bitcast_fusion
  0.7 1.1 fusion.2.refs_0_
  1.8 4.5 %collective-permute-start.1 = (bf16[1,128,2176]{2,1,0:T(8,128)(2,1)S(1)}, bf16[1,128,2176]{2,1,0:T(8,128)(2,1)S(1)}, u32[]{:S(2)}, u32[]{:S(2)}) collective-permute-start(bf16[1,128,2176]{2,1,0:T(8,128)(2,1)S(1)} %fusion.2.refs_0_), channel_id=1, source_target_pairs={{0,64},{1,65},{2,66},{3,67},{4,6},{5,7},{6,4},{7,5},{8,72},{9,73},... | collective-permute-start | bytes 1671176 | tf_op jit(solution)/shard_map/ring/ppermute | solution.py:55
  6.3 0.7 collective-permute-start.2
  7.0 1.9 %collective-permute-start.3 = (bf16[1,128,2176]{2,1,0:T(8,128)(2,1)S(1)}, bf16[1,128,2176]{2,1,0:T(8,128)(2,1)S(1)}, u32[]{:S(2)}, u32[]{:S(2)}) collective-permute-start(bf16[1,128,2176]{2,1,0:T(8,128)(2,1)S(1)} %fusion.2.refs_0_), channel_id=1, source_target_pairs={{0,96},{1,97},{2,98},{3,99},{4,7},{5,4},{6,5},{7,6},{8,104},{9,105... | collective-permute-start | bytes 1671176 | tf_op jit(solution)/shard_map/ring/ppermute | solution.py:55
  9.0 1.3 collective-permute-start
  10.3 1.4 %collective-permute-start.6 = (bf16[1,128,2176]{2,1,0:T(8,128)(2,1)S(1)}, bf16[1,128,2176]{2,1,0:T(8,128)(2,1)S(1)}, u32[]{:S(2)}, u32[]{:S(2)}) collective-permute-start(bf16[1,128,2176]{2,1,0:T(8,128)(2,1)S(1)} %fusion.2.refs_0_), channel_id=1, source_target_pairs={{0,24},{1,25},{2,26},{3,27},{4,28},{5,29},{6,30},{7,31},{8,0},{9,1... | collective-permute-start | bytes 1671176 | tf_op jit(solution)/shard_map/own/ppermute | solution.py:55
  11.7 1.8 %collective-permute-done.1.refs_1_ = bf16[1,128,2176]{2,1,0:T(8,128)(2,1)S(1)} collective-permute-done((bf16[1,128,2176]{2,1,0:T(8,128)(2,1)S(1)}, bf16[1,128,2176]{2,1,0:T(8,128)(2,1)S(1)}, u32[]{:S(2)}, u32[]{:S(2)}) %collective-permute-start.1) | collective-permute-done | bytes 557088 | tf_op jit(solution)/shard_map/ring/ppermute | solution.py:55
  13.5 5.9 %collective-permute-done.2.refs_2_ = bf16[1,128,2176]{2,1,0:T(8,128)(2,1)S(1)} collective-permute-done((bf16[1,128,2176]{2,1,0:T(8,128)(2,1)S(1)}, bf16[1,128,2176]{2,1,0:T(8,128)(2,1)S(1)}, u32[]{:S(2)}, u32[]{:S(2)}) %collective-permute-start.2) | collective-permute-done | bytes 557088 | tf_op jit(solution)/shard_map/ring/ppermute | solution.py:55
  19.5 0.8 collective-permute-done.3.refs_3_
  20.2 0.2 pad_maximum_fusion
  20.5 1.4 collective-permute-start.4
  21.8 1.5 %collective-permute-start.5 = (bf16[3,128,2176]{2,1,0:T(8,128)(2,1)S(1)}, bf16[3,128,2176]{2,1,0:T(8,128)(2,1)S(1)}, u32[]{:S(2)}, u32[]{:S(2)}) collective-permute-start(bf16[3,128,2176]{2,1,0:T(8,128)(2,1)S(1)} %pad_maximum_fusion), channel_id=1, source_target_pairs={{0,24},{1,25},{2,26},{3,27},{4,28},{5,29},{6,30},{7,31},{8,0},{9,1... | collective-permute-start | bytes 5013512 | tf_op jit(solution)/shard_map/near/ppermute | solution.py:55
  23.4 0.7 dynamic-slice_bitcast_fusion
  24.0 0.0 collective-permute-done.refs_4_
  24.0 0.0 collective-permute-done.6.refs_5_
  24.0 0.1 broadcast_in_dim.12.experts_ref
  24.1 2.2 %pack_rows.3 = (bf16[2,144,2048]{2,1,0:T(8,128)(2,1)S(1)}, bf16[2,144,2048]{2,1,0:T(8,128)(2,1)S(1)}, bf16[2,144,2048]{2,1,0:T(8,128)(2,1)S(1)}, bf16[2,144,2048]{2,1,0:T(8,128)(2,1)S(1)}) custom-call(s32[8,128]{1,0:T(8,128)S(1)} %broadcast_in_dim.12.experts_ref, bf16[1,128,2176]{2,1,0:T(8,128)(2,1)S(1)} %fusion.2.refs_0_, ...), custom_call_target="tpu_custom_call" | custom-call | flops 603979776 | bytes 7864320 | tf_op jit(solution)/shard_map/pack_rows/pallas_call | solution.py:104
  26.3 2.8 %collective-permute-start.7 = (bf16[2,144,2048]{2,1,0:T(8,128)(2,1)S(1)}, bf16[2,144,2048]{2,1,0:T(8,128)(2,1)S(1)}, u32[]{:S(2)}, u32[]{:S(2)}) collective-permute-start(bf16[2,144,2048]{2,1,0:T(8,128)(2,1)S(1)} %get-tuple-element.50), channel_id=1, source_target_pairs={{0,2},{1,3},{2,0},{3,1},{4,68},{5,69},{6,70},{7,71},{8,10},{9,11},... | collective-permute-start | bytes 3538952 | tf_op jit(solution)/shard_map/F/ppermute | solution.py:55
  29.1 0.3 collective-permute-start.8
  29.5 2.4 %collective-permute-start.9 = (bf16[2,144,2048]{2,1,0:T(8,128)(2,1)S(1)}, bf16[2,144,2048]{2,1,0:T(8,128)(2,1)S(1)}, u32[]{:S(2)}, u32[]{:S(2)}) collective-permute-start(bf16[2,144,2048]{2,1,0:T(8,128)(2,1)S(1)} %get-tuple-element.52), channel_id=1, source_target_pairs={{0,3},{1,0},{2,1},{3,2},{4,100},{5,101},{6,102},{7,103},{8,11},{9,... | collective-permute-start | bytes 3538952 | tf_op jit(solution)/shard_map/F/ppermute | solution.py:55
  31.8 11.5 %collective-permute-done.7.refs_1_ = bf16[2,144,2048]{2,1,0:T(8,128)(2,1)S(1)} collective-permute-done((bf16[2,144,2048]{2,1,0:T(8,128)(2,1)S(1)}, bf16[2,144,2048]{2,1,0:T(8,128)(2,1)S(1)}, u32[]{:S(2)}, u32[]{:S(2)}) %collective-permute-start.7) | collective-permute-done | bytes 1179680 | tf_op jit(solution)/shard_map/F/ppermute | solution.py:55
  43.3 12.6 %collective-permute-done.8.refs_2_ = bf16[2,144,2048]{2,1,0:T(8,128)(2,1)S(1)} collective-permute-done((bf16[2,144,2048]{2,1,0:T(8,128)(2,1)S(1)}, bf16[2,144,2048]{2,1,0:T(8,128)(2,1)S(1)}, u32[]{:S(2)}, u32[]{:S(2)}) %collective-permute-start.8) | collective-permute-done | bytes 1179680 | tf_op jit(solution)/shard_map/F/ppermute | solution.py:55
  55.9 0.1 collective-permute-done.9.refs_3_
  56.0 0.0 copy-done.1
  56.0 0.0 copy-done
  56.0 5.6 %hidden_gram.6.refs_6_ = f32[776,768]{1,0:T(8,128)S(1)} custom-call(bf16[2,144,2048]{2,1,0:T(8,128)(2,1)S(1)} %get-tuple-element.55.refs_0_, bf16[2,144,2048]{2,1,0:T(8,128)(2,1)S(1)} %collective-permute-done.7.refs_1_, bf16[2,144,2048]{2,1,0:T(8,128)(2,1)S(1)} %collective-permute-done.8.refs_2_, bf16[2,144,2048]{2,1,0:T(8,128)(2,1)S(1)} %collective-permute-done.9.refs_3_, ...), custom_call_target="tpu_custom_call" | custom-call | flops 4303355904 | bytes 13369344 | tf_op jit(solution)/shard_map/hidden_gram/pallas_call | solution.py:162
  61.6 0.0 collective-permute-done.4.refs_0_
  61.6 0.0 collective-permute-done.5.refs_1_
  61.6 2.9 %collective-permute-start.12 = (bf16[1,2048,768]{2,1,0:T(8,128)(2,1)S(1)}, bf16[1,2048,768]{2,1,0:T(8,128)(2,1)S(1)}, u32[]{:S(2)}, u32[]{:S(2)}) collective-permute-start(bf16[1,2048,768]{2,1,0:T(8,128)(2,1)S(1)} %copy-done), channel_id=1, source_target_pairs={{0,4},{1,5},{2,6},{3,7},{4,0},{5,1},{6,2},{7,3},{8,12},{9,13},{10,... | collective-permute-start | bytes 9437192 | tf_op jit(solution)/shard_map/og/ppermute | solution.py:55
  64.5 0.3 collective-permute-start.13
  64.9 2.2 %pack_rows.4 = (bf16[2,144,2048]{2,1,0:T(8,128)(2,1)S(1)}, bf16[2,144,2048]{2,1,0:T(8,128)(2,1)S(1)}, bf16[2,144,2048]{2,1,0:T(8,128)(2,1)S(1)}, bf16[2,144,2048]{2,1,0:T(8,128)(2,1)S(1)}) custom-call(s32[8,128]{1,0:T(8,128)S(1)} %broadcast_in_dim.12.experts_ref, bf16[3,128,2176]{2,1,0:T(8,128)(2,1)S(1)} %collective-permute-done.4.refs_0_, ...), custom_call_target="tpu_custom_call" | custom-call | flops 603979776 | bytes 7864320 | tf_op jit(solution)/shard_map/pack_rows/pallas_call | solution.py:104
  67.1 1.8 %collective-permute-start.14 = (bf16[2,144,2048]{2,1,0:T(8,128)(2,1)S(1)}, bf16[2,144,2048]{2,1,0:T(8,128)(2,1)S(1)}, u32[]{:S(2)}, u32[]{:S(2)}) collective-permute-start(bf16[2,144,2048]{2,1,0:T(8,128)(2,1)S(1)} %get-tuple-element.62), channel_id=1, source_target_pairs={{0,2},{1,3},{2,0},{3,1},{4,68},{5,69},{6,70},{7,71},{8,10},{9,11},... | collective-permute-start | bytes 3538952 | tf_op jit(solution)/shard_map/F/ppermute | solution.py:55
  68.8 1.2 collective-permute-start.15
  70.0 1.5 %collective-permute-start.16 = (bf16[2,144,2048]{2,1,0:T(8,128)(2,1)S(1)}, bf16[2,144,2048]{2,1,0:T(8,128)(2,1)S(1)}, u32[]{:S(2)}, u32[]{:S(2)}) collective-permute-start(bf16[2,144,2048]{2,1,0:T(8,128)(2,1)S(1)} %get-tuple-element.64), channel_id=1, source_target_pairs={{0,3},{1,0},{2,1},{3,2},{4,100},{5,101},{6,102},{7,103},{8,11},{9,... | collective-permute-start | bytes 3538952 | tf_op jit(solution)/shard_map/F/ppermute | solution.py:55
  71.5 0.1 pad_maximum_fusion.1
  71.6 0.1 slice.7
  71.7 0.0 collective-permute-done.12.refs_4_
  71.7 0.2 collective-permute-start.10
  71.9 2.4 %collective-permute-done.13.refs_5_ = bf16[1,2048,768]{2,1,0:T(8,128)(2,1)S(1)} collective-permute-done((bf16[1,2048,768]{2,1,0:T(8,128)(2,1)S(1)}, bf16[1,2048,768]{2,1,0:T(8,128)(2,1)S(1)}, u32[]{:S(2)}, u32[]{:S(2)}) %collective-permute-start.13) | collective-permute-done | bytes 3145760 | tf_op jit(solution)/shard_map/ou/ppermute | solution.py:55
  74.3 2.0 %collective-permute-start.11 = (bf16[2,128,2176]{2,1,0:T(8,128)(2,1)S(1)}, bf16[2,128,2176]{2,1,0:T(8,128)(2,1)S(1)}, u32[]{:S(2)}, u32[]{:S(2)}) collective-permute-start(bf16[2,128,2176]{2,1,0:T(8,128)(2,1)S(1)} %slice.7), channel_id=1, source_target_pairs={{0,24},{1,25},{2,26},{3,27},{4,28},{5,29},{6,30},{7,31},{8,0},{9,1... | collective-permute-start | bytes 3342344 | tf_op jit(solution)/shard_map/far/ppermute | solution.py:55
  76.3 5.6 %hidden_gram.7.refs_6_ = f32[776,768]{1,0:T(8,128)S(1)} custom-call(bf16[2,144,2048]{2,1,0:T(8,128)(2,1)S(1)} %get-tuple-element.55.refs_0_, bf16[2,144,2048]{2,1,0:T(8,128)(2,1)S(1)} %collective-permute-done.7.refs_1_, bf16[2,144,2048]{2,1,0:T(8,128)(2,1)S(1)} %collective-permute-done.8.refs_2_, bf16[2,144,2048]{2,1,0:T(8,128)(2,1)S(1)} %collective-permute-done.9.refs_3_, ...), custom_call_target="tpu_custom_call" | custom-call | flops 4303355904 | bytes 13369344 | tf_op jit(solution)/shard_map/hidden_gram/pallas_call | solution.py:162
  81.9 16.0 %collective-permute-done.10.refs_0_ = bf16[2,128,2176]{2,1,0:T(8,128)(2,1)S(1)} collective-permute-done((bf16[2,128,2176]{2,1,0:T(8,128)(2,1)S(1)}, bf16[2,128,2176]{2,1,0:T(8,128)(2,1)S(1)}, u32[]{:S(2)}, u32[]{:S(2)}) %collective-permute-start.10) | collective-permute-done | bytes 1114144 | tf_op jit(solution)/shard_map/far/ppermute | solution.py:55
  97.9 2.2 %collective-permute-done.11.refs_1_ = bf16[2,128,2176]{2,1,0:T(8,128)(2,1)S(1)} collective-permute-done((bf16[2,128,2176]{2,1,0:T(8,128)(2,1)S(1)}, bf16[2,128,2176]{2,1,0:T(8,128)(2,1)S(1)}, u32[]{:S(2)}, u32[]{:S(2)}) %collective-permute-start.11) | collective-permute-done | bytes 1114144 | tf_op jit(solution)/shard_map/far/ppermute | solution.py:55
  100.1 0.0 collective-permute-done.14.refs_1_
  100.1 0.0 collective-permute-done.15.refs_2_
  100.1 0.0 collective-permute-done.16.refs_3_
  100.1 1.5 %pack_rows.5 = (bf16[2,96,2048]{2,1,0:T(8,128)(2,1)S(1)}, bf16[2,96,2048]{2,1,0:T(8,128)(2,1)S(1)}, bf16[2,96,2048]{2,1,0:T(8,128)(2,1)S(1)}, bf16[2,96,2048]{2,1,0:T(8,128)(2,1)S(1)}) custom-call(s32[8,128]{1,0:T(8,128)S(1)} %broadcast_in_dim.12.experts_ref, bf16[2,128,2176]{2,1,0:T(8,128)(2,1)S(1)} %collective-permute-done.10.refs_0_, ...), custom_call_target="tpu_custom_call" | custom-call | flops 402653184 | bytes 5242880 | tf_op jit(solution)/shard_map/pack_rows/pallas_call | solution.py:104
  101.6 1.8 %collective-permute-start.17 = (bf16[2,96,2048]{2,1,0:T(8,128)(2,1)S(1)}, bf16[2,96,2048]{2,1,0:T(8,128)(2,1)S(1)}, u32[]{:S(2)}, u32[]{:S(2)}) collective-permute-start(bf16[2,96,2048]{2,1,0:T(8,128)(2,1)S(1)} %get-tuple-element.74), channel_id=1, source_target_pairs={{0,2},{1,3},{2,0},{3,1},{4,68},{5,69},{6,70},{7,71},{8,10},{9,11},... | collective-permute-start | bytes 2359304 | tf_op jit(solution)/shard_map/F/ppermute | solution.py:55
  103.4 1.2 collective-permute-start.18
  104.6 1.5 %collective-permute-start.19 = (bf16[2,96,2048]{2,1,0:T(8,128)(2,1)S(1)}, bf16[2,96,2048]{2,1,0:T(8,128)(2,1)S(1)}, u32[]{:S(2)}, u32[]{:S(2)}) collective-permute-start(bf16[2,96,2048]{2,1,0:T(8,128)(2,1)S(1)} %get-tuple-element.76), channel_id=1, source_target_pairs={{0,3},{1,0},{2,1},{3,2},{4,100},{5,101},{6,102},{7,103},{8,11},{9,... | collective-permute-start | bytes 2359304 | tf_op jit(solution)/shard_map/F/ppermute | solution.py:55
  106.1 5.6 %hidden_gram.8.refs_6_ = f32[776,768]{1,0:T(8,128)S(1)} custom-call(bf16[2,144,2048]{2,1,0:T(8,128)(2,1)S(1)} %get-tuple-element.65.refs_0_, bf16[2,144,2048]{2,1,0:T(8,128)(2,1)S(1)} %collective-permute-done.14.refs_1_, bf16[2,144,2048]{2,1,0:T(8,128)(2,1)S(1)} %collective-permute-done.15.refs_2_, ...), custom_call_target="tpu_custom_call" | custom-call | flops 4303355904 | bytes 13369344 | tf_op jit(solution)/shard_map/hidden_gram/pallas_call | solution.py:162
  111.7 5.6 %hidden_gram.9.refs_6_ = f32[776,768]{1,0:T(8,128)S(1)} custom-call(bf16[2,144,2048]{2,1,0:T(8,128)(2,1)S(1)} %get-tuple-element.65.refs_0_, bf16[2,144,2048]{2,1,0:T(8,128)(2,1)S(1)} %collective-permute-done.14.refs_1_, bf16[2,144,2048]{2,1,0:T(8,128)(2,1)S(1)} %collective-permute-done.15.refs_2_, ...), custom_call_target="tpu_custom_call" | custom-call | flops 4303355904 | bytes 13369344 | tf_op jit(solution)/shard_map/hidden_gram/pallas_call | solution.py:162
  117.3 0.0 collective-permute-done.17.refs_1_
  117.3 5.5 %collective-permute-done.18.refs_2_ = bf16[2,96,2048]{2,1,0:T(8,128)(2,1)S(1)} collective-permute-done((bf16[2,96,2048]{2,1,0:T(8,128)(2,1)S(1)}, bf16[2,96,2048]{2,1,0:T(8,128)(2,1)S(1)}, u32[]{:S(2)}, u32[]{:S(2)}) %collective-permute-start.18) | collective-permute-done | bytes 786464 | tf_op jit(solution)/shard_map/F/ppermute | solution.py:55
  122.8 0.0 collective-permute-done.19.refs_3_
  122.8 4.1 %hidden_gram.11 = f32[776,768]{1,0:T(8,128)S(1)} custom-call(bf16[2,96,2048]{2,1,0:T(8,128)(2,1)S(1)} %get-tuple-element.77.refs_0_, bf16[2,96,2048]{2,1,0:T(8,128)(2,1)S(1)} %collective-permute-done.17.refs_1_, bf16[2,96,2048]{2,1,0:T(8,128)(2,1)S(1)} %collective-permute-done.18.refs_2_, bf16[2,96,2048]{2,1,0:T(8,128)(2,1)S(1)} %collective-permute-done.19.refs_3_, ...), custom_call_target="tpu_custom_call" | custom-call | flops 2868903936 | bytes 12582912 | tf_op jit(solution)/shard_map/hidden_gram/pallas_call | solution.py:162
  126.9 0.0 slice-start.1
  126.9 2.4 %collective-permute-start.20 = (f32[776,768]{1,0:T(8,128)S(1)}, f32[776,768]{1,0:T(8,128)S(1)}, u32[]{:S(2)}, u32[]{:S(2)}) collective-permute-start(f32[776,768]{1,0:T(8,128)S(1)} %hidden_gram.11), channel_id=1, source_target_pairs={{0,4},{1,5},{2,6},{3,7},{4,0},{5,1},{6,2},{7,3},{8,12},{9,13},{10,... | collective-permute-start | bytes 7151624 | tf_op jit(solution)/shard_map/sums/ppermute | solution.py:55
  129.3 4.1 %hidden_gram.10.one_ref = f32[776,768]{1,0:T(8,128)S(1)} custom-call(bf16[2,96,2048]{2,1,0:T(8,128)(2,1)S(1)} %get-tuple-element.77.refs_0_, bf16[2,96,2048]{2,1,0:T(8,128)(2,1)S(1)} %collective-permute-done.17.refs_1_, bf16[2,96,2048]{2,1,0:T(8,128)(2,1)S(1)} %collective-permute-done.18.refs_2_, bf16[2,96,2048]{2,1,0:T(8,128)(2,1)S(1)} %collective-permute-done.19.refs_3_, ...), custom_call_target="tpu_custom_call" | custom-call | flops 2868903936 | bytes 12582912 | tf_op jit(solution)/shard_map/hidden_gram/pallas_call | solution.py:162
  133.4 0.1 collective-permute-done.20.two_ref
  133.5 0.0 slice-done
  133.5 0.0 slice-done.1
  133.5 5.5 %mean_product.1 = f32[1,768,2048]{2,1,0:T(8,128)} custom-call(f32[776,768]{1,0:T(8,128)S(1)} %hidden_gram.10.one_ref, f32[776,768]{1,0:T(8,128)S(1)} %collective-permute-done.20.two_ref, f32[1,768,2048]{2,1,0:T(8,128)S(1)} %bitcast.7), custom_call_target="tpu_custom_call" | custom-call | tf_op jit(solution)/shard_map/mean_product/pallas_call | solution.py:199
  (5 shorter events, 0.0 us)
Async XLA Ops:
  1.8 11.8 %collective-permute-start.1 = (bf16[1,128,2176]{2,1,0:T(8,128)(2,1)S(1)}, bf16[1,128,2176]{2,1,0:T(8,128)(2,1)S(1)}, u32[]{:S(2)}, u32[]{:S(2)}) collective-permute-start(bf16[1,128,2176]{2,1,0:T(8,128)(2,1)S(1)} %fusion.2.refs_0_), channel_id=1, source_target_pairs={{0,64},{1,65},{2,66},{3,67},{4,6},{5,7},{6,4},{7,5},{8,72},{9,73},... | collective-permute-start | bytes 1671176 | tf_op jit(solution)/shard_map/ring/ppermute | solution.py:55
  6.3 13.2 %collective-permute-start.2 = (bf16[1,128,2176]{2,1,0:T(8,128)(2,1)S(1)}, bf16[1,128,2176]{2,1,0:T(8,128)(2,1)S(1)}, u32[]{:S(2)}, u32[]{:S(2)}) collective-permute-start(bf16[1,128,2176]{2,1,0:T(8,128)(2,1)S(1)} %fusion.2.refs_0_), channel_id=1, source_target_pairs={{0,32},{1,33},{2,34},{3,35},{4,5},{5,6},{6,7},{7,4},{8,40},{9,41},... | collective-permute-start | bytes 1671176 | tf_op jit(solution)/shard_map/ring/ppermute | solution.py:55
  7.0 13.2 %collective-permute-start.3 = (bf16[1,128,2176]{2,1,0:T(8,128)(2,1)S(1)}, bf16[1,128,2176]{2,1,0:T(8,128)(2,1)S(1)}, u32[]{:S(2)}, u32[]{:S(2)}) collective-permute-start(bf16[1,128,2176]{2,1,0:T(8,128)(2,1)S(1)} %fusion.2.refs_0_), channel_id=1, source_target_pairs={{0,96},{1,97},{2,98},{3,99},{4,7},{5,4},{6,5},{7,6},{8,104},{9,105... | collective-permute-start | bytes 1671176 | tf_op jit(solution)/shard_map/ring/ppermute | solution.py:55
  9.0 15.1 %collective-permute-start = (bf16[1,128,2176]{2,1,0:T(8,128)(2,1)S(1)}, bf16[1,128,2176]{2,1,0:T(8,128)(2,1)S(1)}, u32[]{:S(2)}, u32[]{:S(2)}) collective-permute-start(bf16[1,128,2176]{2,1,0:T(8,128)(2,1)S(1)} %fusion.2.refs_0_), channel_id=1, source_target_pairs={{0,8},{1,9},{2,10},{3,11},{4,12},{5,13},{6,14},{7,15},{8,16},{9,17... | collective-permute-start | bytes 1671176 | tf_op jit(solution)/shard_map/own/ppermute | solution.py:55
  10.3 13.8 %collective-permute-start.6 = (bf16[1,128,2176]{2,1,0:T(8,128)(2,1)S(1)}, bf16[1,128,2176]{2,1,0:T(8,128)(2,1)S(1)}, u32[]{:S(2)}, u32[]{:S(2)}) collective-permute-start(bf16[1,128,2176]{2,1,0:T(8,128)(2,1)S(1)} %fusion.2.refs_0_), channel_id=1, source_target_pairs={{0,24},{1,25},{2,26},{3,27},{4,28},{5,29},{6,30},{7,31},{8,0},{9,1... | collective-permute-start | bytes 1671176 | tf_op jit(solution)/shard_map/own/ppermute | solution.py:55
  20.2 35.8 %copy-start.1 = (bf16[1,2048,768]{2,1,0:T(8,128)(2,1)S(1)}, bf16[1,2048,768]{2,1,0:T(8,128)(2,1)}, u32[]{:S(2)}) copy-start(bf16[1,2048,768]{2,1,0:T(8,128)(2,1)} %refs_5_.5) | copy-start | bytes 9437188
  20.5 41.2 %collective-permute-start.4 = (bf16[3,128,2176]{2,1,0:T(8,128)(2,1)S(1)}, bf16[3,128,2176]{2,1,0:T(8,128)(2,1)S(1)}, u32[]{:S(2)}, u32[]{:S(2)}) collective-permute-start(bf16[3,128,2176]{2,1,0:T(8,128)(2,1)S(1)} %pad_maximum_fusion), channel_id=1, source_target_pairs={{0,8},{1,9},{2,10},{3,11},{4,12},{5,13},{6,14},{7,15},{8,16},{9,17... | collective-permute-start | bytes 5013512 | tf_op jit(solution)/shard_map/near/ppermute | solution.py:55
  21.8 39.8 %collective-permute-start.5 = (bf16[3,128,2176]{2,1,0:T(8,128)(2,1)S(1)}, bf16[3,128,2176]{2,1,0:T(8,128)(2,1)S(1)}, u32[]{:S(2)}, u32[]{:S(2)}) collective-permute-start(bf16[3,128,2176]{2,1,0:T(8,128)(2,1)S(1)} %pad_maximum_fusion), channel_id=1, source_target_pairs={{0,24},{1,25},{2,26},{3,27},{4,28},{5,29},{6,30},{7,31},{8,0},{9,1... | collective-permute-start | bytes 5013512 | tf_op jit(solution)/shard_map/near/ppermute | solution.py:55
  24.1 31.9 %copy-start = (bf16[1,2048,768]{2,1,0:T(8,128)(2,1)S(1)}, bf16[1,2048,768]{2,1,0:T(8,128)(2,1)}, u32[]{:S(2)}) copy-start(bf16[1,2048,768]{2,1,0:T(8,128)(2,1)} %refs_4_.5) | copy-start | bytes 9437188
  26.3 17.0 %collective-permute-start.7 = (bf16[2,144,2048]{2,1,0:T(8,128)(2,1)S(1)}, bf16[2,144,2048]{2,1,0:T(8,128)(2,1)S(1)}, u32[]{:S(2)}, u32[]{:S(2)}) collective-permute-start(bf16[2,144,2048]{2,1,0:T(8,128)(2,1)S(1)} %get-tuple-element.50), channel_id=1, source_target_pairs={{0,2},{1,3},{2,0},{3,1},{4,68},{5,69},{6,70},{7,71},{8,10},{9,11},... | collective-permute-start | bytes 3538952 | tf_op jit(solution)/shard_map/F/ppermute | solution.py:55
  29.1 26.8 %collective-permute-start.8 = (bf16[2,144,2048]{2,1,0:T(8,128)(2,1)S(1)}, bf16[2,144,2048]{2,1,0:T(8,128)(2,1)S(1)}, u32[]{:S(2)}, u32[]{:S(2)}) collective-permute-start(bf16[2,144,2048]{2,1,0:T(8,128)(2,1)S(1)} %get-tuple-element.51), channel_id=1, source_target_pairs={{0,1},{1,2},{2,3},{3,0},{4,36},{5,37},{6,38},{7,39},{8,9},{9,10},{... | collective-permute-start | bytes 3538952 | tf_op jit(solution)/shard_map/F/ppermute | solution.py:55
  29.5 26.6 %collective-permute-start.9 = (bf16[2,144,2048]{2,1,0:T(8,128)(2,1)S(1)}, bf16[2,144,2048]{2,1,0:T(8,128)(2,1)S(1)}, u32[]{:S(2)}, u32[]{:S(2)}) collective-permute-start(bf16[2,144,2048]{2,1,0:T(8,128)(2,1)S(1)} %get-tuple-element.52), channel_id=1, source_target_pairs={{0,3},{1,0},{2,1},{3,2},{4,100},{5,101},{6,102},{7,103},{8,11},{9,... | collective-permute-start | bytes 3538952 | tf_op jit(solution)/shard_map/F/ppermute | solution.py:55
  61.6 10.1 %collective-permute-start.12 = (bf16[1,2048,768]{2,1,0:T(8,128)(2,1)S(1)}, bf16[1,2048,768]{2,1,0:T(8,128)(2,1)S(1)}, u32[]{:S(2)}, u32[]{:S(2)}) collective-permute-start(bf16[1,2048,768]{2,1,0:T(8,128)(2,1)S(1)} %copy-done), channel_id=1, source_target_pairs={{0,4},{1,5},{2,6},{3,7},{4,0},{5,1},{6,2},{7,3},{8,12},{9,13},{10,... | collective-permute-start | bytes 9437192 | tf_op jit(solution)/shard_map/og/ppermute | solution.py:55
  64.5 9.8 %collective-permute-start.13 = (bf16[1,2048,768]{2,1,0:T(8,128)(2,1)S(1)}, bf16[1,2048,768]{2,1,0:T(8,128)(2,1)S(1)}, u32[]{:S(2)}, u32[]{:S(2)}) collective-permute-start(bf16[1,2048,768]{2,1,0:T(8,128)(2,1)S(1)} %copy-done.1), channel_id=1, source_target_pairs={{0,4},{1,5},{2,6},{3,7},{4,0},{5,1},{6,2},{7,3},{8,12},{9,13},{10,... | collective-permute-start | bytes 9437192 | tf_op jit(solution)/shard_map/ou/ppermute | solution.py:55
  67.1 33.0 %collective-permute-start.14 = (bf16[2,144,2048]{2,1,0:T(8,128)(2,1)S(1)}, bf16[2,144,2048]{2,1,0:T(8,128)(2,1)S(1)}, u32[]{:S(2)}, u32[]{:S(2)}) collective-permute-start(bf16[2,144,2048]{2,1,0:T(8,128)(2,1)S(1)} %get-tuple-element.62), channel_id=1, source_target_pairs={{0,2},{1,3},{2,0},{3,1},{4,68},{5,69},{6,70},{7,71},{8,10},{9,11},... | collective-permute-start | bytes 3538952 | tf_op jit(solution)/shard_map/F/ppermute | solution.py:55
  68.8 31.3 %collective-permute-start.15 = (bf16[2,144,2048]{2,1,0:T(8,128)(2,1)S(1)}, bf16[2,144,2048]{2,1,0:T(8,128)(2,1)S(1)}, u32[]{:S(2)}, u32[]{:S(2)}) collective-permute-start(bf16[2,144,2048]{2,1,0:T(8,128)(2,1)S(1)} %get-tuple-element.63), channel_id=1, source_target_pairs={{0,1},{1,2},{2,3},{3,0},{4,36},{5,37},{6,38},{7,39},{8,9},{9,10},{... | collective-permute-start | bytes 3538952 | tf_op jit(solution)/shard_map/F/ppermute | solution.py:55
  70.0 30.1 %collective-permute-start.16 = (bf16[2,144,2048]{2,1,0:T(8,128)(2,1)S(1)}, bf16[2,144,2048]{2,1,0:T(8,128)(2,1)S(1)}, u32[]{:S(2)}, u32[]{:S(2)}) collective-permute-start(bf16[2,144,2048]{2,1,0:T(8,128)(2,1)S(1)} %get-tuple-element.64), channel_id=1, source_target_pairs={{0,3},{1,0},{2,1},{3,2},{4,100},{5,101},{6,102},{7,103},{8,11},{9,... | collective-permute-start | bytes 3538952 | tf_op jit(solution)/shard_map/F/ppermute | solution.py:55
  71.7 26.2 %collective-permute-start.10 = (bf16[2,128,2176]{2,1,0:T(8,128)(2,1)S(1)}, bf16[2,128,2176]{2,1,0:T(8,128)(2,1)S(1)}, u32[]{:S(2)}, u32[]{:S(2)}) collective-permute-start(bf16[2,128,2176]{2,1,0:T(8,128)(2,1)S(1)} %pad_maximum_fusion.1), channel_id=1, source_target_pairs={{0,8},{1,9},{2,10},{3,11},{4,12},{5,13},{6,14},{7,15},{8,16},{9,17... | collective-permute-start | bytes 3342344 | tf_op jit(solution)/shard_map/far/ppermute | solution.py:55
  74.3 25.8 %collective-permute-start.11 = (bf16[2,128,2176]{2,1,0:T(8,128)(2,1)S(1)}, bf16[2,128,2176]{2,1,0:T(8,128)(2,1)S(1)}, u32[]{:S(2)}, u32[]{:S(2)}) collective-permute-start(bf16[2,128,2176]{2,1,0:T(8,128)(2,1)S(1)} %slice.7), channel_id=1, source_target_pairs={{0,24},{1,25},{2,26},{3,27},{4,28},{5,29},{6,30},{7,31},{8,0},{9,1... | collective-permute-start | bytes 3342344 | tf_op jit(solution)/shard_map/far/ppermute | solution.py:55
  101.6 15.7 %collective-permute-start.17 = (bf16[2,96,2048]{2,1,0:T(8,128)(2,1)S(1)}, bf16[2,96,2048]{2,1,0:T(8,128)(2,1)S(1)}, u32[]{:S(2)}, u32[]{:S(2)}) collective-permute-start(bf16[2,96,2048]{2,1,0:T(8,128)(2,1)S(1)} %get-tuple-element.74), channel_id=1, source_target_pairs={{0,2},{1,3},{2,0},{3,1},{4,68},{5,69},{6,70},{7,71},{8,10},{9,11},... | collective-permute-start | bytes 2359304 | tf_op jit(solution)/shard_map/F/ppermute | solution.py:55
  103.4 19.4 %collective-permute-start.18 = (bf16[2,96,2048]{2,1,0:T(8,128)(2,1)S(1)}, bf16[2,96,2048]{2,1,0:T(8,128)(2,1)S(1)}, u32[]{:S(2)}, u32[]{:S(2)}) collective-permute-start(bf16[2,96,2048]{2,1,0:T(8,128)(2,1)S(1)} %get-tuple-element.75), channel_id=1, source_target_pairs={{0,1},{1,2},{2,3},{3,0},{4,36},{5,37},{6,38},{7,39},{8,9},{9,10},{... | collective-permute-start | bytes 2359304 | tf_op jit(solution)/shard_map/F/ppermute | solution.py:55
  104.6 18.2 %collective-permute-start.19 = (bf16[2,96,2048]{2,1,0:T(8,128)(2,1)S(1)}, bf16[2,96,2048]{2,1,0:T(8,128)(2,1)S(1)}, u32[]{:S(2)}, u32[]{:S(2)}) collective-permute-start(bf16[2,96,2048]{2,1,0:T(8,128)(2,1)S(1)} %get-tuple-element.76), channel_id=1, source_target_pairs={{0,3},{1,0},{2,1},{3,2},{4,100},{5,101},{6,102},{7,103},{8,11},{9,... | collective-permute-start | bytes 2359304 | tf_op jit(solution)/shard_map/F/ppermute | solution.py:55
  122.8 10.7 %slice-start = ((s8[6291456]{0:T(1024)(128)(4,1)}), s8[4194304]{0:T(1024)(128)(4,1)S(1)}, s32[]{:S(2)}) async-start(s8[6291456]{0:T(1024)(128)(4,1)} %bitcast.6), calls=%async_computation | async-start | bytes 8388608
  126.9 6.6 %slice-start.1 = ((s8[6291456]{0:T(1024)(128)(4,1)}), s8[2097152]{0:T(1024)(128)(4,1)S(1)}, s32[]{:S(2)}) async-start(s8[6291456]{0:T(1024)(128)(4,1)} %bitcast.6), calls=%async_computation.1 | async-start | bytes 4194304
  126.9 6.6 %collective-permute-start.20 = (f32[776,768]{1,0:T(8,128)S(1)}, f32[776,768]{1,0:T(8,128)S(1)}, u32[]{:S(2)}, u32[]{:S(2)}) collective-permute-start(f32[776,768]{1,0:T(8,128)S(1)} %hidden_gram.11), channel_id=1, source_target_pairs={{0,4},{1,5},{2,6},{3,7},{4,0},{5,1},{6,2},{7,3},{8,12},{9,13},{10,... | collective-permute-start | bytes 7151624 | tf_op jit(solution)/shard_map/sums/ppermute | solution.py:55
